TPU v7x, 32 devices: a whole 2x2x4 slice. The times are simulated.
32 devices in a mesh: groups: 2 (over y), col: 16 (over z, x, core).
Axes of the slice: x: 2, y: 2, z: 4, core: 2. Of those that a mesh axis runs over, the one named last changes fastest.
Arguments:
- features: bfloat16 [16, 128, 768], P('groups', 'col'), parts along dimension 0, may hold values from -6 to 6
- column_table: bfloat16 [128, 768], P('col'), may hold values from -3 to 3
- dw_kernel: bfloat16 [7, 7, 768], replicated, may hold values from -0.875 to 0.875
- norm_gain: float32 [768], replicated, may hold values from 0.5 to 2
- expand_weight: bfloat16 [768, 3072], replicated, may hold values from -0.21875 to 0.21875
- reduce_weight: bfloat16 [3072, 768], replicated, may hold values from -0.109375 to 0.109375
- layer_scale: float32 [768], replicated, may hold values from 0.2 to 1
Outputs:
- disagreement: bfloat16 [16, 128, 768], P('groups', 'col'), parts along dimension 0
- grad_expand: float32 [1536, 3072], P(('groups', 'col')), parts along dimension 0
- grad_reduce: float32 [6144, 768], P(('groups', 'col')), parts along dimension 0
- grad_kernel: float32 [14, 7, 768], P('groups'), parts along dimension 0
- grad_gain: float32 [1536], P('groups'), parts along dimension 0
- grad_scale: float32 [1536], P('groups'), parts along dimension 0
There are 2 independent parts, one for each index of `groups`. A program takes and returns all parts, laid end to end along the dimension named above; an argument that names none is the same for every part. Nothing has to cross between parts.
All inputs are finite; a program needn't handle non-finite values.
Results may differ from a plain program's by a relative error of at most 0.0096.
The roundings to bfloat16 on the way count: a program that leaves them out, or rounds other values in their place, can miss the bound.
Values may be sent and summed in bfloat16 or wider, within the bound.
A program may use at most 128 MiB of HBM per device.

v0:
```python
import math

import jax
import jax.numpy as jnp
from jax import lax
from jax.sharding import PartitionSpec as P


def swapped(block, axis, bit):
    count = lax.axis_size(axis)
    route = []
    for low in range(count):
        high = low | 1 << bit
        if high != low and high < count:
            route += [(low, high), (high, low)]
    return lax.ppermute(block, axis, route)


def padded_2(block, sides, width):
    for axis, dim in sides:
        count = lax.axis_size(axis)
        forward = [(i, i + 1) for i in range(count - 1)]
        backward = [(target, source) for source, target in forward]
        low = lax.ppermute(
            lax.slice_in_dim(block, block.shape[dim] - width, None, axis=dim), axis, forward
        )
        high = lax.ppermute(lax.slice_in_dim(block, 0, width, axis=dim), axis, backward)
        block = jnp.concatenate([low, block, high], axis=dim)
    return block


def gelu_parts(pre):
    normal_cdf = 0.5 * (1.0 + jax.scipy.special.erf(pre * 0.7071067811865476))
    density = jnp.exp(-0.5 * pre * pre) * 0.3989422804014327
    return (pre * normal_cdf, normal_cdf + pre * density)


def mirror_slab(slab_part):
    for bit_index in range(lax.axis_size("col").bit_length() - 1):
        slab_part = swapped(slab_part, "col", bit_index)
    return slab_part


def on_device(
    features, column_table, dw_kernel, norm_gain, expand_weight, reduce_weight, layer_scale
):
    row_count, col_count, channels = features.shape
    slab_count = lax.axis_size("col")
    total_cols = col_count * slab_count
    table_f = column_table.astype(jnp.float32)
    kernel_f = dw_kernel.astype(jnp.float32)
    flipped = mirror_slab(features)[:, ::-1]
    second_view = flipped.astype(jnp.float32) + table_f
    kernels = jnp.stack([kernel_f, kernel_f])
    first_view = features.astype(jnp.float32) + table_f
    stacked_views = jnp.stack([first_view, second_view]).astype(jnp.bfloat16)
    widened = padded_2(stacked_views, (("col", 2),), 3)
    padded = jnp.pad(widened.astype(jnp.float32), ((0, 0), (3, 3), (0, 0), (0, 0)))
    conv = jnp.zeros((2, row_count, col_count, channels), jnp.float32)
    for row_off in range(7):
        for col_off in range(7):
            weights_here = kernels[:, row_off, col_off][:, None, None, :]
            conv = (
                conv
                + weights_here
                * padded[:, row_off : row_off + row_count, col_off : col_off + col_count]
            )
    mean_val = jnp.mean(conv, axis=-1, keepdims=True)
    centred = conv - mean_val
    variance = jnp.mean(centred * centred, axis=-1, keepdims=True)
    inverse = lax.rsqrt(variance + 1e-06)
    nhat = centred * inverse
    normed = (nhat * norm_gain).astype(jnp.bfloat16).reshape(-1, channels)
    pre = jnp.dot(normed, expand_weight, preferred_element_type=jnp.float32)
    activated, gelu_slope = gelu_parts(pre)
    hidden = activated.astype(jnp.bfloat16)
    branch = jnp.dot(hidden, reduce_weight, preferred_element_type=jnp.float32)
    outputs = (stacked_views.astype(jnp.float32) + layer_scale * branch.reshape(conv.shape)).astype(
        jnp.bfloat16
    )
    partner_out = mirror_slab(outputs[1])[:, ::-1]
    difference = outputs[0].astype(jnp.float32) - partner_out.astype(jnp.float32)
    disagreement = difference.astype(jnp.bfloat16)
    residual = (difference * (1.0 / math.sqrt(row_count * total_cols))).astype(jnp.bfloat16)
    residual = lax.optimization_barrier(residual)
    returned = -mirror_slab(residual)[:, ::-1]
    out_grads = jnp.stack([residual, returned]).astype(jnp.float32)
    flat_grad = out_grads.reshape(-1, channels)
    grad_scale_local = jnp.sum(branch * flat_grad, axis=0)
    dbranch = (layer_scale * flat_grad).astype(jnp.bfloat16)
    grad_reduce = lax.psum_scatter(
        lax.dot_general(
            hidden, dbranch, (((0,), (0,)), ((), ())), preferred_element_type=jnp.float32
        ),
        "col",
        scatter_dimension=0,
        tiled=True,
    )
    dhidden = lax.dot_general(
        dbranch, reduce_weight, (((1,), (1,)), ((), ())), preferred_element_type=jnp.float32
    )
    dpre = (dhidden * gelu_slope).astype(jnp.bfloat16)
    grad_expand = lax.psum_scatter(
        lax.dot_general(normed, dpre, (((0,), (0,)), ((), ())), preferred_element_type=jnp.float32),
        "col",
        scatter_dimension=0,
        tiled=True,
    )
    dnormed = lax.dot_general(
        dpre, expand_weight, (((1,), (1,)), ((), ())), preferred_element_type=jnp.float32
    ).reshape(conv.shape)
    grad_gain_local = jnp.sum(dnormed * nhat, axis=(0, 1, 2))
    scaled = dnormed * norm_gain
    dconv = inverse * (
        scaled
        - jnp.mean(scaled, axis=-1, keepdims=True)
        - nhat * jnp.mean(scaled * nhat, axis=-1, keepdims=True)
    )
    kernel_rows = []
    for row_off in range(7):
        kernel_cols = []
        for col_off in range(7):
            window = padded[:, row_off : row_off + row_count, col_off : col_off + col_count]
            kernel_cols.append(jnp.sum(window * dconv, axis=(1, 2)))
        kernel_rows.append(jnp.stack(kernel_cols, axis=1))
    view_kernels = jnp.stack(kernel_rows, axis=1)
    kernel_local = view_kernels[0] + view_kernels[1]
    grad_kernel, grad_gain, grad_scale = lax.psum(
        (kernel_local, grad_gain_local, grad_scale_local), "col"
    )
    return (disagreement, grad_expand, grad_reduce, grad_kernel, grad_gain, grad_scale)


def solution(mesh):
    in_specs = (P("groups", "col", None), P("col", None), P(), P(), P(), P(), P())
    out_specs = (
        P("groups", "col", None),
        P(("groups", "col"), None),
        P(("groups", "col"), None),
        P("groups", None, None),
        P("groups"),
        P("groups"),
    )
    return jax.shard_map(
        on_device, mesh=mesh, in_specs=in_specs, out_specs=out_specs, check_vma=False
    )
```

profile of v0, /device:TPU:0, one launch (start us, length us, event | category | flops | bytes accessed | tf_op | source)
XLA Modules:
  0.0 435.2 jit_solution(12626554175668020912)
XLA Ops:
  14.5 2.6 collective-permute-start.1
  17.0 3.4 collective-permute-done.1
  20.5 1.8 collective-permute-start.2
  22.3 2.8 collective-permute-done.2
  25.1 2.8 collective-permute-start.3
  28.7 2.0 collective-permute-done.3
  33.6 3.8 collective-permute-done.5
  37.6 2.9 fusion.16
  44.3 3.3 collective-permute-start.6
  48.6 2.6 collective-permute-start.7
  51.2 3.3 collective-permute-done.7
  56.0 3.1 collective-permute-done.8
  59.1 3.4 collective-permute-start.9
  62.5 3.8 collective-permute-done.9
  66.3 3.4 rev.10
  69.7 1.6 multiply_convert_fusion.2
  72.8 1.7 collective-permute-start.11
  74.5 3.2 collective-permute-done.11
  77.9 4.3 collective-permute-done.12
  82.3 1.9 collective-permute-start.13
  84.2 4.6 %collective-permute-done.13 = bf16[8,8,768]{2,1,0:T(8,128)(2,1)S(1)} collective-permute-done((bf16[8,8,768]{2,1,0:T(8,128)(2,1)S(1)}, bf16[8,8,768]{2,1,0:T(8,128)(2,1)S(1)}, u32[]{:S(2)}, u32[]{:S(2)}) %collective-permute-start.13) | collective-permute-done | bytes 98336 | tf_op jit(solution)/shard_map/ppermute | solution.py:16
  91.5 4.1 fusion
  95.6 1.8 multiply_reduce_fusion.51
  99.2 1.5 multiply_reduce_fusion
  100.7 1.8 multiply_reduce_fusion.1
  106.5 5.1 %fusion.14 = f32[3072,768]{1,0:T(8,128)} fusion(bf16[128,768]{1,0:T(8,128)(2,1)S(1)} %get-tuple-element.65, f32[128,3072]{1,0:T(8,128)S(1)} %fusion.17), kind=kOutput, calls=%fused_computation.244 | convolution fusion | flops 605945856 | bytes 11206656 | tf_op jit(solution)/shard_map/dot_general | solution.py:92
  112.7 5.1 %fusion.18 = f32[768,3072]{1,0:T(8,128)} fusion(bf16[128,768]{1,0:T(8,128)(2,1)S(1)} %bitcast.163, bf16[128,3072]{1,0:T(8,128)(2,1)S(1)} %copy-done.3), kind=kOutput, calls=%fused_computation.248 | convolution fusion | flops 603979776 | bytes 10420224 | tf_op jit(solution)/shard_map/dot_general | solution.py:104
  118.4 30.6 %all-reduce.1 = (f32[768]{0:T(1024)}, f32[768]{0:T(1024)}) all-reduce(f32[768]{0:T(1024)S(1)} %copy-done.9, f32[768]{0:T(1024)S(1)} %copy-done.8), channel_id=1, replica_groups=mesh['groups'=2,'col'=16] {'col'}, use_global_device_ids=true, to_apply=%region_57.58 | all-reduce | flops 1536 | bytes 12288 | tf_op jit(solution)/shard_map/psum | solution.py:128
  149.0 45.0 %all-reduce.4.cloned.1.call-done = f32[7,7,768]{2,1,0:T(8,128)} async-done(((f32[7,7,768]{2,1,0:T(8,128)}), f32[7,7,768]{2,1,0:T(8,128)}) %all-reduce.4.cloned.1.call-update) | async-done | bytes 150544 | tf_op jit(solution)/shard_map/psum | solution.py:128
  194.0 116.7 %reduce-scatter.5.cloned.1.call-done = f32[192,768]{1,0:T(8,128)} async-done(((f32[3072,768]{1,0:T(8,128)}), f32[192,768]{1,0:T(8,128)}) %reduce-scatter.5.cloned.1.call-update) | async-done | bytes 589840 | tf_op jit(solution)/shard_map/reduce_scatter | solution.py:91
  310.7 116.4 %reduce-scatter.3.cloned.1.call-done = f32[48,3072]{1,0:T(8,128)} async-done(((f32[768,3072]{1,0:T(8,128)}), f32[48,3072]{1,0:T(8,128)}) %reduce-scatter.3.cloned.1.call-update) | async-done | bytes 589840 | tf_op jit(solution)/shard_map/reduce_scatter | solution.py:103
  427.1 1.6 copy.119
  (158 shorter events, 28.6 us)
Async XLA Ops:
  7.2 23.6 %copy-start.4 = (bf16[8,8,768]{2,1,0:T(8,128)(2,1)S(1)}, bf16[8,8,768]{2,1,0:T(8,128)(2,1)}, u32[]{:S(2)}) copy-start(bf16[8,8,768]{2,1,0:T(8,128)(2,1)} %param.7) | copy-start | bytes 294916
  7.2 186.8 %all-reduce.4.cloned.1.call-start = ((), (), s32[]{:S(2)}) async-start(), calls=%async_computation.4 | async-start | bytes 344064 | tf_op jit(solution)/shard_map/psum | solution.py:128
  7.2 7.2 %collective-permute-start = (bf16[8,8,768]{2,1,0:T(8,128)(2,1)}, bf16[8,8,768]{2,1,0:T(8,128)(2,1)S(1)}, u32[]{:S(2)}, u32[]{:S(2)}) collective-permute-start(bf16[8,8,768]{2,1,0:T(8,128)(2,1)} %param.7), channel_id=1, source_target_pairs={{0,1},{1,0},{2,3},{3,2},{4,5},{5,4},{6,7},{7,6},{8,9},{9,8},{10,11... | collective-permute-start | bytes 294920 | tf_op jit(solution)/shard_map/ppermute | solution.py:16
  14.5 6.0 %collective-permute-start.1 = (bf16[8,8,768]{2,1,0:T(8,128)(2,1)S(1)}, bf16[8,8,768]{2,1,0:T(8,128)(2,1)S(1)}, u32[]{:S(2)}, u32[]{:S(2)}) collective-permute-start(bf16[8,8,768]{2,1,0:T(8,128)(2,1)S(1)} %collective-permute-done), channel_id=1, source_target_pairs={{0,2},{2,0},{1,3},{3,1},{4,6},{6,4},{5,7},{7,5},{8,10},{10,8},{9,1... | collective-permute-start | bytes 294920 | tf_op jit(solution)/shard_map/ppermute | solution.py:16
  20.5 4.6 %collective-permute-start.2 = (bf16[8,8,768]{2,1,0:T(8,128)(2,1)S(1)}, bf16[8,8,768]{2,1,0:T(8,128)(2,1)S(1)}, u32[]{:S(2)}, u32[]{:S(2)}) collective-permute-start(bf16[8,8,768]{2,1,0:T(8,128)(2,1)S(1)} %collective-permute-done.1), channel_id=1, source_target_pairs={{0,4},{4,0},{1,5},{5,1},{2,6},{6,2},{3,7},{7,3},{8,12},{12,8},{9,1... | collective-permute-start | bytes 294920 | tf_op jit(solution)/shard_map/ppermute | solution.py:16
  25.1 5.5 %collective-permute-start.3 = (bf16[8,8,768]{2,1,0:T(8,128)(2,1)S(1)}, bf16[8,8,768]{2,1,0:T(8,128)(2,1)S(1)}, u32[]{:S(2)}, u32[]{:S(2)}) collective-permute-start(bf16[8,8,768]{2,1,0:T(8,128)(2,1)S(1)} %collective-permute-done.2), channel_id=1, source_target_pairs={{0,8},{8,0},{1,9},{9,1},{2,10},{10,2},{3,11},{11,3},{4,12},{12,4},... | collective-permute-start | bytes 294920 | tf_op jit(solution)/shard_map/ppermute | solution.py:16
  31.0 2.6 collective-permute-start.4
  32.3 5.2 %collective-permute-start.5 = (bf16[2,8,3,768]{3,2,1,0:T(4,128)(2,1)S(1)}, bf16[2,8,3,768]{3,2,1,0:T(4,128)(2,1)S(1)}, u32[]{:S(2)}, u32[]{:S(2)}) collective-permute-start(bf16[2,8,3,768]{3,2,1,0:T(4,128)(2,1)S(1)} %get-tuple-element.67), channel_id=1, source_target_pairs={{1,0},{2,1},{3,2},{4,3},{5,4},{6,5},{7,6},{8,7},{9,8},{10,9},{11,1... | collective-permute-start | bytes 221192 | tf_op jit(solution)/shard_map/ppermute | solution.py:27
  37.6 3.2 copy-start.5
  37.6 3.3 copy-start
  40.9 2.3 copy-start.1
  43.3 1.0 copy-start.7
  44.3 4.2 collective-permute-start.6
  48.6 5.9 %collective-permute-start.7 = (bf16[8,8,768]{2,1,0:T(8,128)(2,1)S(1)}, bf16[8,8,768]{2,1,0:T(8,128)(2,1)S(1)}, u32[]{:S(2)}, u32[]{:S(2)}) collective-permute-start(bf16[8,8,768]{2,1,0:T(8,128)(2,1)S(1)} %collective-permute-done.6), channel_id=1, source_target_pairs={{0,2},{2,0},{1,3},{3,1},{4,6},{6,4},{5,7},{7,5},{8,10},{10,8},{9,1... | collective-permute-start | bytes 294920 | tf_op jit(solution)/shard_map/ppermute | solution.py:16
  54.5 4.6 %collective-permute-start.8 = (bf16[8,8,768]{2,1,0:T(8,128)(2,1)S(1)}, bf16[8,8,768]{2,1,0:T(8,128)(2,1)S(1)}, u32[]{:S(2)}, u32[]{:S(2)}) collective-permute-start(bf16[8,8,768]{2,1,0:T(8,128)(2,1)S(1)} %collective-permute-done.7), channel_id=1, source_target_pairs={{0,4},{4,0},{1,5},{5,1},{2,6},{6,2},{3,7},{7,3},{8,12},{12,8},{9,1... | collective-permute-start | bytes 294920 | tf_op jit(solution)/shard_map/ppermute | solution.py:16
  59.1 7.2 %collective-permute-start.9 = (bf16[8,8,768]{2,1,0:T(8,128)(2,1)S(1)}, bf16[8,8,768]{2,1,0:T(8,128)(2,1)}, u32[]{:S(2)}, u32[]{:S(2)}) collective-permute-start(bf16[8,8,768]{2,1,0:T(8,128)(2,1)S(1)} %collective-permute-done.8), channel_id=1, source_target_pairs={{0,8},{8,0},{1,9},{9,1},{2,10},{10,2},{3,11},{11,3},{4,12},{12,4},... | collective-permute-start | bytes 294920 | tf_op jit(solution)/shard_map/ppermute | solution.py:16
  71.3 1.5 collective-permute-start.10
  72.8 4.9 %collective-permute-start.11 = (bf16[8,8,768]{2,1,0:T(8,128)(2,1)S(1)}, bf16[8,8,768]{2,1,0:T(8,128)(2,1)S(1)}, u32[]{:S(2)}, u32[]{:S(2)}) collective-permute-start(bf16[8,8,768]{2,1,0:T(8,128)(2,1)S(1)} %collective-permute-done.10), channel_id=1, source_target_pairs={{0,2},{2,0},{1,3},{3,1},{4,6},{6,4},{5,7},{7,5},{8,10},{10,8},{9,1... | collective-permute-start | bytes 294920 | tf_op jit(solution)/shard_map/ppermute | solution.py:16
  77.6 4.6 %collective-permute-start.12 = (bf16[8,8,768]{2,1,0:T(8,128)(2,1)S(1)}, bf16[8,8,768]{2,1,0:T(8,128)(2,1)S(1)}, u32[]{:S(2)}, u32[]{:S(2)}) collective-permute-start(bf16[8,8,768]{2,1,0:T(8,128)(2,1)S(1)} %collective-permute-done.11), channel_id=1, source_target_pairs={{0,4},{4,0},{1,5},{5,1},{2,6},{6,2},{3,7},{7,3},{8,12},{12,8},{9,1... | collective-permute-start | bytes 294920 | tf_op jit(solution)/shard_map/ppermute | solution.py:16
  82.3 6.6 %collective-permute-start.13 = (bf16[8,8,768]{2,1,0:T(8,128)(2,1)S(1)}, bf16[8,8,768]{2,1,0:T(8,128)(2,1)S(1)}, u32[]{:S(2)}, u32[]{:S(2)}) collective-permute-start(bf16[8,8,768]{2,1,0:T(8,128)(2,1)S(1)} %collective-permute-done.12), channel_id=1, source_target_pairs={{0,8},{8,0},{1,9},{9,1},{2,10},{10,2},{3,11},{11,3},{4,12},{12,4},... | collective-permute-start | bytes 294920 | tf_op jit(solution)/shard_map/ppermute | solution.py:16
  89.9 5.6 %slice-start = ((s8[4718592]{0:T(1024)(128)(4,1)}), s8[4194304]{0:T(1024)(128)(4,1)S(1)}, s32[]{:S(2)}) async-start(s8[4718592]{0:T(1024)(128)(4,1)} %bitcast.152), calls=%async_computation.5 | async-start | bytes 8388608
  91.4 4.1 slice-start.1
  91.5 4.1 copy-start.6
  95.6 1.8 copy-start.2
  106.2 204.5 %reduce-scatter.5.cloned.1.call-start = ((), (), s32[]{:S(2)}) async-start(), calls=%async_computation.3 | async-start | bytes 10027008 | tf_op jit(solution)/shard_map/reduce_scatter | solution.py:91
  111.5 1.1 copy-start.3
  111.6 315.6 %reduce-scatter.3.cloned.1.call-start = ((), (), s32[]{:S(2)}) async-start(), calls=%async_computation.2 | async-start | bytes 10027008 | tf_op jit(solution)/shard_map/reduce_scatter | solution.py:103
  117.7 0.7 copy-start.8
  117.7 0.7 copy-start.9
Sparse Core Ops, SparseCore 0:
  106.4 87.5 all-reduce.3
  198.7 112.0 reduce-scatter.4
  316.0 111.1 reduce-scatter.2
where the time goes:
time: 436 us; the launch traced here: 435 us
  waiting for transfers between devices  315 us (72%)
  blocking collectives  30.6 us (7%)
  starting transfers between devices  25.4 us (6%)
  other arithmetic  20.9 us (5%)
  matrix products  17.7 us (4%)
  between operations  14.7 us (3%)
  local copies, waits for them, and re-layouts  11.1 us (3%)
    reduce_scatter x1, waiting for transfers between devices, on_device(): lax.psum_scatter(lax.dot_general(hidden, dbranch, (((0,), (0,)), ((), ())...  117 us
    reduce_scatter x1, waiting for transfers between devices, on_device(): lax.psum_scatter(lax.dot_general(normed, dpre, (((0,), (0,)), ((), ())),...  116 us
    psum x1, waiting for transfers between devices, on_device(): lax.psum((kernel_local, grad_gain_local, grad_scale_local), 'col')  45 us
    ppermute x12, waiting for transfers between devices, swapped(): return lax.ppermute(block, axis, route)  33 us
    psum x1, blocking collectives, on_device(): lax.psum((kernel_local, grad_gain_local, grad_scale_local), 'col')  30.6 us
    ppermute x12, starting transfers between devices, swapped(): return lax.ppermute(block, axis, route)  22.5 us
  transfers between devices with their start and end apart: 17, of which 15 were waited for; matrix products, arithmetic and copies ran while one was open for 4% of the time, Pallas kernels for 0%

commit v1 on v0

v1 whole, which is shorter than its diff:
```python
import math

import jax
import jax.numpy as jnp
from jax import lax
from jax.sharding import PartitionSpec as P


def permuted(block, target):
    count = lax.axis_size("col")
    return lax.ppermute(block, "col", [(i, target(i)) for i in range(count)])


def gelu_parts(pre):
    normal_cdf = 0.5 * (1.0 + jax.scipy.special.erf(pre * 0.7071067811865476))
    density = jnp.exp(-0.5 * pre * pre) * 0.3989422804014327
    return (pre * normal_cdf, normal_cdf + pre * density)


def with_halo(block, width):
    count = lax.axis_size("col")
    forward = [(i, i + 1) for i in range(count - 1)]
    backward = [(target, source) for source, target in forward]
    low = lax.ppermute(block[:, :, -width:], "col", forward)
    high = lax.ppermute(block[:, :, :width], "col", backward)
    return jnp.concatenate([low, block, high], axis=2)


def pick(array, index, axis):
    return lax.dynamic_index_in_dim(array, index, axis, keepdims=False)


def outer_scatter(partial):
    outer = partial.shape[0]
    count = lax.axis_size("col")
    mine = lax.axis_index("col") // 4
    rounded = partial.astype(jnp.bfloat16)
    total = pick(partial, mine, 0)
    for step in range(1, outer):
        block = pick(rounded, lax.rem(mine + step, outer), 0)
        got = permuted(block, lambda i: (i + 4 * step) % count)
        total = total + got.astype(jnp.float32)
    return total


def all_sum(block):
    count = lax.axis_size("col")
    for bit in range(count.bit_length() - 1):
        block = block + permuted(block, lambda i: i ^ (1 << bit))
    return block


def on_device(
    features, column_table, dw_kernel, norm_gain, expand_weight, reduce_weight, layer_scale
):
    row_count, col_count, channels = features.shape
    count = lax.axis_size("col")
    outer = count // 4
    me = lax.axis_index("col")
    core = lax.rem(me, 2)
    side = lax.rem(me // 2, 2)
    total_cols = col_count * count
    hidden_size = expand_weight.shape[1]
    pixels = row_count * col_count

    mirrored_table = permuted(column_table, lambda i: count - 1 - i)[::-1]
    tables = jnp.stack([column_table, mirrored_table]).astype(jnp.float32)
    views = (features.astype(jnp.float32)[None] + tables[:, None]).astype(jnp.bfloat16)
    kernel_f = dw_kernel.astype(jnp.float32)
    kernels = jnp.stack([kernel_f, kernel_f[:, ::-1]])
    widened = with_halo(views, 3)
    padded = jnp.pad(widened.astype(jnp.float32), ((0, 0), (3, 3), (0, 0), (0, 0)))
    conv = jnp.zeros((2, row_count, col_count, channels), jnp.float32)
    for row_off in range(7):
        for col_off in range(7):
            weights_here = kernels[:, row_off, col_off][:, None, None, :]
            conv = (
                conv
                + weights_here
                * padded[:, row_off : row_off + row_count, col_off : col_off + col_count]
            )
    mean_val = jnp.mean(conv, axis=-1, keepdims=True)
    centred = conv - mean_val
    variance = jnp.mean(centred * centred, axis=-1, keepdims=True)
    inverse = lax.rsqrt(variance + 1e-06)
    nhat = centred * inverse
    normed = (nhat * norm_gain).astype(jnp.bfloat16).reshape(-1, channels)
    pre = jnp.dot(normed, expand_weight, preferred_element_type=jnp.float32)
    activated, gelu_slope = gelu_parts(pre)
    hidden = activated.astype(jnp.bfloat16)
    branch = jnp.dot(hidden, reduce_weight, preferred_element_type=jnp.float32)
    outputs = (views.astype(jnp.float32) + layer_scale * branch.reshape(conv.shape)).astype(
        jnp.bfloat16
    )
    difference = outputs[0].astype(jnp.float32) - outputs[1].astype(jnp.float32)
    disagreement = difference.astype(jnp.bfloat16)
    residual = (difference * (1.0 / math.sqrt(row_count * total_cols))).astype(jnp.bfloat16)
    residual = lax.optimization_barrier(residual)
    flat_grad = residual.astype(jnp.float32).reshape(pixels, channels)
    branches = branch.reshape(2, pixels, channels)
    grad_scale_local = jnp.sum((branches[0] - branches[1]) * flat_grad, axis=0)
    dbranch = (layer_scale * flat_grad).astype(jnp.bfloat16)

    hiddens = hidden.astype(jnp.float32).reshape(2, pixels, hidden_size)
    contrast = (hiddens[0] - hiddens[1]).astype(jnp.bfloat16)
    contrast_t = contrast.T.reshape(outer, 2, 2, hidden_size // count, pixels)
    other_core = lambda i: i ^ 1
    other_side = lambda i: i ^ 2
    contrast_pair = jnp.concatenate(
        [pick(contrast_t, core, 2), permuted(pick(contrast_t, 1 - core, 2), other_core)], axis=-1
    )
    dbranch_pair = jnp.concatenate([dbranch, permuted(dbranch, other_core)], axis=0)
    contrast_quad = jnp.concatenate(
        [pick(contrast_pair, side, 1), permuted(pick(contrast_pair, 1 - side, 1), other_side)],
        axis=-1,
    )
    dbranch_quad = jnp.concatenate([dbranch_pair, permuted(dbranch_pair, other_side)], axis=0)
    reduce_quad = jnp.dot(
        contrast_quad.reshape(-1, 4 * pixels), dbranch_quad, preferred_element_type=jnp.float32
    ).reshape(outer, hidden_size // count, channels)
    grad_reduce = outer_scatter(reduce_quad)

    dhidden = lax.dot_general(
        dbranch, reduce_weight, (((1,), (1,)), ((), ())), preferred_element_type=jnp.float32
    )
    slopes = gelu_slope.reshape(2, pixels, hidden_size)
    dpre = jnp.stack([dhidden * slopes[0], -dhidden * slopes[1]]).astype(jnp.bfloat16)
    dpre = dpre.reshape(2 * pixels, hidden_size)

    normed_t = normed.T.reshape(outer, 2, 2, channels // count, 2 * pixels)
    normed_pair = jnp.concatenate(
        [pick(normed_t, core, 2), permuted(pick(normed_t, 1 - core, 2), other_core)], axis=-1
    )
    dpre_pair = jnp.concatenate([dpre, permuted(dpre, other_core)], axis=0)

    def expand_part(which):
        rows = pick(normed_pair, which, 1).reshape(-1, 4 * pixels)
        return jnp.dot(rows, dpre_pair, preferred_element_type=jnp.float32)

    sent = permuted(expand_part(1 - side).astype(jnp.bfloat16), other_side)
    expand_quad = expand_part(side) + sent.astype(jnp.float32)
    grad_expand = outer_scatter(expand_quad.reshape(outer, channels // count, hidden_size))

    dnormed = lax.dot_general(
        dpre, expand_weight, (((1,), (1,)), ((), ())), preferred_element_type=jnp.float32
    ).reshape(conv.shape)
    grad_gain_local = jnp.sum(dnormed * nhat, axis=(0, 1, 2))
    scaled = dnormed * norm_gain
    dconv = inverse * (
        scaled
        - jnp.mean(scaled, axis=-1, keepdims=True)
        - nhat * jnp.mean(scaled * nhat, axis=-1, keepdims=True)
    )
    kernel_rows = []
    for row_off in range(7):
        kernel_cols = []
        for col_off in range(7):
            window = padded[:, row_off : row_off + row_count, col_off : col_off + col_count]
            kernel_cols.append(jnp.sum(window * dconv, axis=(1, 2)))
        kernel_rows.append(jnp.stack(kernel_cols, axis=1))
    view_kernels = jnp.stack(kernel_rows, axis=1)
    kernel_local = view_kernels[0] + view_kernels[1][:, ::-1]
    small = jnp.concatenate(
        [kernel_local.reshape(49, channels), grad_gain_local[None], grad_scale_local[None]], axis=0
    )
    small = all_sum(small)
    return (
        disagreement,
        grad_expand,
        grad_reduce,
        small[:49].reshape(7, 7, channels),
        small[49],
        small[50],
    )


def solution(mesh):
    in_specs = (P("groups", "col", None), P("col", None), P(), P(), P(), P(), P())
    out_specs = (
        P("groups", "col", None),
        P(("groups", "col"), None),
        P(("groups", "col"), None),
        P("groups", None, None),
        P("groups"),
        P("groups"),
    )
    return jax.shard_map(
        on_device, mesh=mesh, in_specs=in_specs, out_specs=out_specs, check_vma=False
    )
```

time: 436 us -> 180 us (0.41)
  the two profiles are of different devices: /device:TPU:0 before, /device:TPU:8 now
where the time goes in v1:
time: 180 us; the launch traced here: 179 us
  waiting for transfers between devices  62.3 us (35%)
  local copies, waits for them, and re-layouts  45.9 us (26%)
  starting transfers between devices  37.3 us (21%)
  other arithmetic  17.4 us (10%)
  matrix products  14.6 us (8%)
    ppermute x18, waiting for transfers between devices, permuted(): return lax.ppermute(block, 'col', [(i, target(i)) for i in range(count)])  60.2 us
    ppermute x18, starting transfers between devices, permuted(): return lax.ppermute(block, 'col', [(i, target(i)) for i in range(count)])  30.8 us
    another operation x56, local copies, waits for them, and re-layouts, on_device(): kernel_rows.append(jnp.stack(kernel_cols, axis=1))  29.1 us
    unnamed x57, local copies, waits for them, and re-layouts  5.14 us
    dot_general x2, matrix products, expand_part(): return jnp.dot(rows, dpre_pair, preferred_element_type=jnp.float32)  4.63 us
    ppermute x1, starting transfers between devices, with_halo(): high = lax.ppermute(block[:, :, :width], 'col', backward)  3.97 us
  transfers between devices with their start and end apart: 20, of which 11 were waited for; matrix products, arithmetic and copies ran while one was open for 34% of the time, Pallas kernels for 0%

profile of v1, /device:TPU:8, one launch (start us, length us, event | category | flops | bytes accessed | tf_op | source)
XLA Modules:
  0.0 178.9 jit_solution(1798984700636207768)
XLA Ops:
  0.6 2.0 %collective-permute-start = (bf16[8,768]{1,0:T(8,128)(2,1)}, bf16[8,768]{1,0:T(8,128)(2,1)S(1)}, u32[]{:S(2)}, u32[]{:S(2)}) collective-permute-start(bf16[8,768]{1,0:T(8,128)(2,1)} %param.8), channel_id=1, source_target_pairs={{0,15},{1,14},{2,13},{3,12},{4,11},{5,10},{6,9},{7,8},{8,7},{9,6},... | collective-permute-start | bytes 36872 | tf_op jit(solution)/shard_map/ppermute | solution.py:11
  2.6 2.3 %rev.10 = f32[7,7,768]{2,1,0:T(8,128)S(1)} reverse(bf16[7,7,768]{2,1,0:T(8,128)(2,1)} %param.9), dimensions={1} | reverse | bytes 225792 | tf_op jit(solution)/shard_map/rev | solution.py:70
  7.0 2.6 %collective-permute-start.1 = (bf16[2,8,3,768]{3,2,1,0:T(4,128)(2,1)S(1)}, bf16[2,8,3,768]{3,2,1,0:T(4,128)(2,1)S(1)}, u32[]{:S(2)}, u32[]{:S(2)}) collective-permute-start(bf16[2,8,3,768]{3,2,1,0:T(4,128)(2,1)S(1)} %get-tuple-element.133), channel_id=1, source_target_pairs={{0,1},{1,2},{2,3},{3,4},{4,5},{5,6},{6,7},{7,8},{8,9},{9,10},{10,1... | collective-permute-start | bytes 221192 | tf_op jit(solution)/shard_map/ppermute | solution.py:24
  9.6 4.0 %collective-permute-start.2 = (bf16[2,8,3,768]{3,2,1,0:T(4,128)(2,1)S(1)}, bf16[2,8,3,768]{3,2,1,0:T(4,128)(2,1)S(1)}, u32[]{:S(2)}, u32[]{:S(2)}) collective-permute-start(bf16[2,8,3,768]{3,2,1,0:T(4,128)(2,1)S(1)} %get-tuple-element.134), channel_id=1, source_target_pairs={{1,0},{2,1},{3,2},{4,3},{5,4},{6,5},{7,6},{8,7},{9,8},{10,9},{11,1... | collective-permute-start | bytes 221192 | tf_op jit(solution)/shard_map/ppermute | solution.py:25
  14.0 1.8 %collective-permute-done.2 = bf16[2,8,3,768]{3,2,1,0:T(4,128)(2,1)S(1)} collective-permute-done((bf16[2,8,3,768]{3,2,1,0:T(4,128)(2,1)S(1)}, bf16[2,8,3,768]{3,2,1,0:T(4,128)(2,1)S(1)}, u32[]{:S(2)}, u32[]{:S(2)}) %collective-permute-start.2) | collective-permute-done | bytes 73760 | tf_op jit(solution)/shard_map/ppermute | solution.py:25
  16.0 2.9 %fusion.42 = (f32[2,8,8]{2,1,0:T(8,128)S(1)}, f32[2,8,8,768]{3,2,1,0:T(8,128)S(1)}) fusion(f32[2,768]{1,0:T(2,128)S(1)} %get-tuple-element.138, f32[2,768]{1,0:T(2,128)S(1)} %get-tuple-element.142, f32[2,768]{1,0:T(2,128)S(1)} %get-tuple-element.143, f32[2,768]{1,0:T(2,128)S(1)} %get-tuple-element.144, f32[2,768]{1,0:T(2,128)S(1)} %get-tuple-element.145, ...), kind=kLoop, calls=%fused_computation.299 | loop fusion | flops 9633664 | bytes 4233728 | tf_op jit(solution)/shard_map/reduce_sum | solution.py:82
  19.3 1.5 fusion.41
  23.7 2.4 %fusion.8 = (bf16[64,3072]{1,0:T(8,128)(2,1)S(1)}, bf16[64,3072]{1,0:T(8,128)(2,1)S(1)}) fusion(f32[128,3072]{1,0:T(8,128)S(1)} %get-tuple-element.67, bf16[64,768]{1,0:T(8,128)(2,1)} %fusion.28, bf16[3072,768]{1,0:T(8,128)(2,1)S(1)} %bitcast.213), kind=kOutput, calls=%fused_computation.59 | convolution fusion | flops 302972928 | bytes 7176192 | tf_op jit(solution)/shard_map/dot_general | solution.py:123
  26.2 2.4 %multiply_reduce_fusion.50 = (f32[2,8,8]{2,1,0:T(8,128)S(1)}, f32[768]{0:T(1024)}, f32[2,8,8]{2,1,0:T(8,128)S(1)}, f32[2,8,8,768]{3,2,1,0:T(8,128)S(1)}) fusion(f32[2,8,8,768]{3,2,1,0:T(8,128)S(1)} %get-tuple-element.64, f32[768]{0:T(1024)S(1)} %copy-done.6, f32[2,8,8]{2,1,0:T(8,128)S(1)} %add_rsqrt_fusion, f32[2,8,8]{2,1,0:T(8,128)S(1)} %broadcast_multiply_fusion.2, ...), kind=kOutput, calls=%fused_computation.136 | convolution fusion | flops 605158400 | bytes 6299648 | tf_op jit(solution)/shard_map/dot_general | solution.py:144
  28.5 1.2 multiply_reduce_fusion.1
  29.7 1.0 multiply_reduce_fusion.19
  66.6 1.1 copy.13
  68.0 1.6 fusion.32
  72.8 2.6 %convolution_convert_fusion = bf16[192,3072]{1,0:T(8,128)(2,1)} fusion(bf16[192,256]{1,0:T(8,128)(2,1)S(1)} %bitcast.239, bf16[128,3072]{1,0:T(8,128)(2,1)} %collective-permute-done.4, bf16[128,3072]{1,0:T(8,128)(2,1)S(1)} %bitcast.228), kind=kOutput, calls=%fused_computation.45 | convolution fusion | flops 305725440 | bytes 2850816 | tf_op jit(solution)/shard_map/dot_general | solution.py:138
  75.4 1.7 collective-permute-start.5
  77.8 1.1 constant_dynamic-slice_fusion
  79.4 1.0 pad_maximum_fusion.4
  81.6 1.8 collective-permute-start.17
  84.1 28.2 %collective-permute-done.17 = f32[51,768]{1,0:T(8,128)S(1)} collective-permute-done((f32[51,768]{1,0:T(8,128)S(1)}, f32[51,768]{1,0:T(8,128)S(1)}, u32[]{:S(2)}, u32[]{:S(2)}) %collective-permute-start.17) | collective-permute-done | bytes 156704 | tf_op jit(solution)/shard_map/ppermute | solution.py:11
  112.3 1.9 %collective-permute-start.18 = (f32[51,768]{1,0:T(8,128)S(1)}, f32[51,768]{1,0:T(8,128)S(1)}, u32[]{:S(2)}, u32[]{:S(2)}) collective-permute-start(f32[51,768]{1,0:T(8,128)S(1)} %add.351), channel_id=1, source_target_pairs={{0,4},{1,5},{2,6},{3,7},{4,0},{5,1},{6,2},{7,3},{8,12},{9,13},{10,... | collective-permute-start | bytes 470024 | tf_op jit(solution)/shard_map/ppermute | solution.py:11
  114.4 3.4 %collective-permute-done.18 = f32[51,768]{1,0:T(8,128)S(1)} collective-permute-done((f32[51,768]{1,0:T(8,128)S(1)}, f32[51,768]{1,0:T(8,128)S(1)}, u32[]{:S(2)}, u32[]{:S(2)}) %collective-permute-start.18) | collective-permute-done | bytes 156704 | tf_op jit(solution)/shard_map/ppermute | solution.py:11
  117.8 3.0 %collective-permute-start.19 = (f32[51,768]{1,0:T(8,128)S(1)}, f32[51,768]{1,0:T(8,128)S(1)}, u32[]{:S(2)}, u32[]{:S(2)}) collective-permute-start(f32[51,768]{1,0:T(8,128)S(1)} %add.352), channel_id=1, source_target_pairs={{0,8},{1,9},{2,10},{3,11},{4,12},{5,13},{6,14},{7,15},{8,0},{9,1},... | collective-permute-start | bytes 470024 | tf_op jit(solution)/shard_map/ppermute | solution.py:11
  120.9 2.8 %fusion.44 = (bf16[4,192,768]{2,1,0:T(8,128)(2,1)S(1)}, f32[4,192,768]{2,1,0:T(8,128)}) fusion(bf16[128,768]{1,0:T(8,128)(2,1)S(1)} %collective-permute-done.12, bf16[64,768]{1,0:T(8,128)(2,1)} %collective-permute-done.11, bf16[64,768]{1,0:T(8,128)(2,1)} %fusion.28, bf16[4,192,128]{2,1,0:T(8,128)(2,1)S(1)} %collective-permute-done.10, ...), kind=kOutput, calls=%fused_computation.301 | convolution fusion | flops 304545792 | bytes 4325376 | tf_op jit(solution)/shard_map/dot_general | solution.py:118
  124.9 3.3 %collective-permute-start.14 = (bf16[192,768]{1,0:T(8,128)(2,1)}, bf16[192,768]{1,0:T(8,128)(2,1)}, u32[]{:S(2)}, u32[]{:S(2)}) collective-permute-start(bf16[192,768]{1,0:T(8,128)(2,1)} %get-tuple-element.70), channel_id=1, source_target_pairs={{0,8},{1,9},{2,10},{3,11},{4,12},{5,13},{6,14},{7,15},{8,0},{9,1},... | collective-permute-start | bytes 884744 | tf_op jit(solution)/shard_map/ppermute | solution.py:11
  128.3 2.0 %convolution_add_fusion = f32[192,3072]{1,0:T(8,128)S(1)} fusion(bf16[192,256]{1,0:T(8,128)(2,1)S(1)} %bitcast.236, bf16[192,3072]{1,0:T(8,128)(2,1)} %collective-permute-done.5, bf16[128,3072]{1,0:T(8,128)(2,1)} %collective-permute-done.4, bf16[128,3072]{1,0:T(8,128)(2,1)S(1)} %bitcast.229), kind=kOutput, calls=%fused_computation.44 | convolution fusion | flops 306315264 | bytes 5210112 | tf_op jit(solution)/shard_map/dot_general | solution.py:138
  131.4 9.8 %collective-permute-start.6 = (bf16[48,3072]{1,0:T(8,128)(2,1)}, bf16[48,3072]{1,0:T(8,128)(2,1)S(1)}, u32[]{:S(2)}, u32[]{:S(2)}) collective-permute-start(bf16[48,3072]{1,0:T(8,128)(2,1)} %get-tuple-element.71), channel_id=1, source_target_pairs={{0,4},{1,5},{2,6},{3,7},{4,8},{5,9},{6,10},{7,11},{8,12},{9,13},{1... | collective-permute-start | bytes 884744 | tf_op jit(solution)/shard_map/ppermute | solution.py:11
  141.2 4.8 %collective-permute-start.7 = (bf16[48,3072]{1,0:T(8,128)(2,1)}, bf16[48,3072]{1,0:T(8,128)(2,1)S(1)}, u32[]{:S(2)}, u32[]{:S(2)}) collective-permute-start(bf16[48,3072]{1,0:T(8,128)(2,1)} %get-tuple-element.73), channel_id=1, source_target_pairs={{0,8},{1,9},{2,10},{3,11},{4,12},{5,13},{6,14},{7,15},{8,0},{9,1},... | collective-permute-start | bytes 884744 | tf_op jit(solution)/shard_map/ppermute | solution.py:11
  147.8 17.9 %collective-permute-done.14 = bf16[192,768]{1,0:T(8,128)(2,1)} collective-permute-done((bf16[192,768]{1,0:T(8,128)(2,1)}, bf16[192,768]{1,0:T(8,128)(2,1)}, u32[]{:S(2)}, u32[]{:S(2)}) %collective-permute-start.14) | collective-permute-done | bytes 294944 | tf_op jit(solution)/shard_map/ppermute | solution.py:11
  166.2 2.3 %fusion.13 = f32[192,768]{1,0:T(8,128)} fusion(bf16[192,768]{1,0:T(8,128)(2,1)} %collective-permute-done.15, bf16[192,768]{1,0:T(8,128)(2,1)} %collective-permute-done.14, bf16[192,768]{1,0:T(8,128)(2,1)} %collective-permute-done.13, f32[4,192,768]{2,1,0:T(8,128)} %get-tuple-element.136, s32[]{:T(128)S(6)} %select_n.55), kind=kLoop, calls=%fused_computation.70 | loop fusion | flops 884736 | bytes 2064388 | tf_op jit(solution)/shard_map/add | solution.py:42
  168.5 3.6 %collective-permute-done.6 = bf16[48,3072]{1,0:T(8,128)(2,1)S(1)} collective-permute-done((bf16[48,3072]{1,0:T(8,128)(2,1)}, bf16[48,3072]{1,0:T(8,128)(2,1)S(1)}, u32[]{:S(2)}, u32[]{:S(2)}) %collective-permute-start.6) | collective-permute-done | bytes 294944 | tf_op jit(solution)/shard_map/ppermute | solution.py:11
  172.1 5.1 %collective-permute-done.7 = bf16[48,3072]{1,0:T(8,128)(2,1)S(1)} collective-permute-done((bf16[48,3072]{1,0:T(8,128)(2,1)}, bf16[48,3072]{1,0:T(8,128)(2,1)S(1)}, u32[]{:S(2)}, u32[]{:S(2)}) %collective-permute-start.7) | collective-permute-done | bytes 294944 | tf_op jit(solution)/shard_map/ppermute | solution.py:11
  178.0 1.0 fusion.15
  (187 shorter events, 53.5 us)
Async XLA Ops:
  0.6 6.1 %collective-permute-start = (bf16[8,768]{1,0:T(8,128)(2,1)}, bf16[8,768]{1,0:T(8,128)(2,1)S(1)}, u32[]{:S(2)}, u32[]{:S(2)}) collective-permute-start(bf16[8,768]{1,0:T(8,128)(2,1)} %param.8), channel_id=1, source_target_pairs={{0,15},{1,14},{2,13},{3,12},{4,11},{5,10},{6,9},{7,8},{8,7},{9,6},... | collective-permute-start | bytes 36872 | tf_op jit(solution)/shard_map/ppermute | solution.py:11
  5.8 0.9 copy-start.5
  5.8 1.1 copy-start.9
  7.0 6.9 %collective-permute-start.1 = (bf16[2,8,3,768]{3,2,1,0:T(4,128)(2,1)S(1)}, bf16[2,8,3,768]{3,2,1,0:T(4,128)(2,1)S(1)}, u32[]{:S(2)}, u32[]{:S(2)}) collective-permute-start(bf16[2,8,3,768]{3,2,1,0:T(4,128)(2,1)S(1)} %get-tuple-element.133), channel_id=1, source_target_pairs={{0,1},{1,2},{2,3},{3,4},{4,5},{5,6},{6,7},{7,8},{8,9},{9,10},{10,1... | collective-permute-start | bytes 221192 | tf_op jit(solution)/shard_map/ppermute | solution.py:24
  9.6 6.2 %collective-permute-start.2 = (bf16[2,8,3,768]{3,2,1,0:T(4,128)(2,1)S(1)}, bf16[2,8,3,768]{3,2,1,0:T(4,128)(2,1)S(1)}, u32[]{:S(2)}, u32[]{:S(2)}) collective-permute-start(bf16[2,8,3,768]{3,2,1,0:T(4,128)(2,1)S(1)} %get-tuple-element.134), channel_id=1, source_target_pairs={{1,0},{2,1},{3,2},{4,3},{5,4},{6,5},{7,6},{8,7},{9,8},{10,9},{11,1... | collective-permute-start | bytes 221192 | tf_op jit(solution)/shard_map/ppermute | solution.py:25
  15.8 3.3 %copy-start.6 = (f32[768]{0:T(1024)S(1)}, f32[768]{0:T(1024)}, u32[]{:S(2)}) copy-start(f32[768]{0:T(1024)} %param.10) | copy-start | bytes 9220
  16.0 3.3 %copy-start = (bf16[768,3072]{1,0:T(8,128)(2,1)S(1)}, bf16[768,3072]{1,0:T(8,128)(2,1)}, u32[]{:S(2)}) copy-start(bf16[768,3072]{1,0:T(8,128)(2,1)} %param.11) | copy-start | bytes 14155780
  19.1 2.3 %slice-start = ((s8[4718592]{0:T(1024)(128)(4,1)}), s8[4194304]{0:T(1024)(128)(4,1)S(1)}, s32[]{:S(2)}) async-start(s8[4718592]{0:T(1024)(128)(4,1)} %bitcast.212), calls=%async_computation | async-start | bytes 8388608
  19.3 1.6 copy-start.1
  19.3 2.2 %slice-start.1 = ((s8[4718592]{0:T(1024)(128)(4,1)}), s8[524288]{0:T(1024)(128)(4,1)S(1)}, s32[]{:S(2)}) async-start(s8[4718592]{0:T(1024)(128)(4,1)} %bitcast.212), calls=%async_computation.1 | async-start | bytes 1048576
  21.5 0.8 copy-start.7
  23.1 3.1 %copy-start.2 = (bf16[8,8,768]{2,1,0:T(8,128)(2,1)}, bf16[8,8,768]{2,1,0:T(8,128)(2,1)S(1)}, u32[]{:S(2)}) copy-start(bf16[8,8,768]{2,1,0:T(8,128)(2,1)S(1)} %get-tuple-element.127) | copy-start | bytes 294916
  31.3 48.0 %collective-permute-start.11 = (bf16[64,768]{1,0:T(8,128)(2,1)}, bf16[64,768]{1,0:T(8,128)(2,1)}, u32[]{:S(2)}, u32[]{:S(2)}) collective-permute-start(bf16[64,768]{1,0:T(8,128)(2,1)} %fusion.28), channel_id=1, source_target_pairs={{0,1},{1,0},{2,3},{3,2},{4,5},{5,4},{6,7},{7,6},{8,9},{9,8},{10,11... | collective-permute-start | bytes 294920 | tf_op jit(solution)/shard_map/ppermute | solution.py:11
  56.2 14.5 %copy-start.8 = (f32[768]{0:T(1024)S(1)}, f32[768]{0:T(1024)}, u32[]{:S(2)}) copy-start(f32[768]{0:T(1024)} %get-tuple-element.56) | copy-start | bytes 9220
  56.2 14.5 %copy-start.3 = (bf16[8,8,768]{2,1,0:T(8,128)(2,1)S(1)}, bf16[8,8,768]{2,1,0:T(8,128)(2,1)}, u32[]{:S(2)}) copy-start(bf16[8,8,768]{2,1,0:T(8,128)(2,1)} %copy-done.2) | copy-start | bytes 294916
  56.2 16.6 %collective-permute-start.4 = (bf16[128,3072]{1,0:T(8,128)(2,1)S(1)}, bf16[128,3072]{1,0:T(8,128)(2,1)}, u32[]{:S(2)}, u32[]{:S(2)}) collective-permute-start(bf16[128,3072]{1,0:T(8,128)(2,1)S(1)} %bitcast.227), channel_id=1, source_target_pairs={{0,1},{1,0},{2,3},{3,2},{4,5},{5,4},{6,7},{7,6},{8,9},{9,8},{10,11... | collective-permute-start | bytes 2359304 | tf_op jit(solution)/shard_map/ppermute | solution.py:11
  70.7 1.4 collective-permute-start.3
  71.5 9.2 %collective-permute-start.16 = (f32[51,768]{1,0:T(8,128)}, f32[51,768]{1,0:T(8,128)}, u32[]{:S(2)}, u32[]{:S(2)}) collective-permute-start(f32[51,768]{1,0:T(8,128)} %pad_maximum_fusion.5), channel_id=1, source_target_pairs={{0,1},{1,0},{2,3},{3,2},{4,5},{5,4},{6,7},{7,6},{8,9},{9,8},{10,11... | collective-permute-start | bytes 470024 | tf_op jit(solution)/shard_map/ppermute | solution.py:11
  75.4 52.9 %collective-permute-start.5 = (bf16[192,3072]{1,0:T(8,128)(2,1)}, bf16[192,3072]{1,0:T(8,128)(2,1)}, u32[]{:S(2)}, u32[]{:S(2)}) collective-permute-start(bf16[192,3072]{1,0:T(8,128)(2,1)} %convolution_convert_fusion), channel_id=1, source_target_pairs={{0,2},{1,3},{2,0},{3,1},{4,6},{5,7},{6,4},{7,5},{8,10},{9,11},{10,... | collective-permute-start | bytes 3538952 | tf_op jit(solution)/shard_map/ppermute | solution.py:11
  79.1 4.4 %collective-permute-start.9 = (bf16[4,2,192,64]{2,3,1,0:T(8,128)(2,1)S(1)}, bf16[4,2,192,64]{2,3,1,0:T(8,128)(2,1)S(1)}, u32[]{:S(2)}, u32[]{:S(2)}) collective-permute-start(bf16[4,2,192,64]{2,3,1,0:T(8,128)(2,1)S(1)} %bitcast.237), channel_id=1, source_target_pairs={{0,1},{1,0},{2,3},{3,2},{4,5},{5,4},{6,7},{7,6},{8,9},{9,8},{10,11... | collective-permute-start | bytes 589832 | tf_op jit(solution)/shard_map/ppermute | solution.py:11
  80.3 40.5 %collective-permute-start.12 = (bf16[128,768]{1,0:T(8,128)(2,1)S(1)}, bf16[128,768]{1,0:T(8,128)(2,1)S(1)}, u32[]{:S(2)}, u32[]{:S(2)}) collective-permute-start(bf16[128,768]{1,0:T(8,128)(2,1)S(1)} %pad_maximum_fusion.4), channel_id=1, source_target_pairs={{0,2},{1,3},{2,0},{3,1},{4,6},{5,7},{6,4},{7,5},{8,10},{9,11},{10,... | collective-permute-start | bytes 589832 | tf_op jit(solution)/shard_map/ppermute | solution.py:11
  81.6 30.7 %collective-permute-start.17 = (f32[51,768]{1,0:T(8,128)S(1)}, f32[51,768]{1,0:T(8,128)S(1)}, u32[]{:S(2)}, u32[]{:S(2)}) collective-permute-start(f32[51,768]{1,0:T(8,128)S(1)} %fusion.54), channel_id=1, source_target_pairs={{0,2},{1,3},{2,0},{3,1},{4,6},{5,7},{6,4},{7,5},{8,10},{9,11},{10,... | collective-permute-start | bytes 470024 | tf_op jit(solution)/shard_map/ppermute | solution.py:11
  83.7 37.2 %collective-permute-start.10 = (bf16[4,192,128]{2,1,0:T(8,128)(2,1)S(1)}, bf16[4,192,128]{2,1,0:T(8,128)(2,1)S(1)}, u32[]{:S(2)}, u32[]{:S(2)}) collective-permute-start(bf16[4,192,128]{2,1,0:T(8,128)(2,1)S(1)} %bitcast.238), channel_id=1, source_target_pairs={{0,2},{1,3},{2,0},{3,1},{4,6},{5,7},{6,4},{7,5},{8,10},{9,11},{10,... | collective-permute-start | bytes 589832 | tf_op jit(solution)/shard_map/ppermute | solution.py:11
  112.3 5.5 %collective-permute-start.18 = (f32[51,768]{1,0:T(8,128)S(1)}, f32[51,768]{1,0:T(8,128)S(1)}, u32[]{:S(2)}, u32[]{:S(2)}) collective-permute-start(f32[51,768]{1,0:T(8,128)S(1)} %add.351), channel_id=1, source_target_pairs={{0,4},{1,5},{2,6},{3,7},{4,0},{5,1},{6,2},{7,3},{8,12},{9,13},{10,... | collective-permute-start | bytes 470024 | tf_op jit(solution)/shard_map/ppermute | solution.py:11
  117.8 10.4 %collective-permute-start.19 = (f32[51,768]{1,0:T(8,128)S(1)}, f32[51,768]{1,0:T(8,128)S(1)}, u32[]{:S(2)}, u32[]{:S(2)}) collective-permute-start(f32[51,768]{1,0:T(8,128)S(1)} %add.352), channel_id=1, source_target_pairs={{0,8},{1,9},{2,10},{3,11},{4,12},{5,13},{6,14},{7,15},{8,0},{9,1},... | collective-permute-start | bytes 470024 | tf_op jit(solution)/shard_map/ppermute | solution.py:11
  123.7 4.6 %copy-start.4 = (bf16[4,1,48,256]{3,2,1,0:T(8,128)(2,1)S(1)}, bf16[4,1,48,256]{3,2,1,0:T(8,128)(2,1)}, u32[]{:S(2)}) copy-start(bf16[4,1,48,256]{3,2,1,0:T(8,128)(2,1)} %get-tuple-element.130) | copy-start | bytes 294916
  124.5 22.0 %collective-permute-start.13 = (bf16[192,768]{1,0:T(8,128)(2,1)S(1)}, bf16[192,768]{1,0:T(8,128)(2,1)}, u32[]{:S(2)}, u32[]{:S(2)}) collective-permute-start(bf16[192,768]{1,0:T(8,128)(2,1)S(1)} %get-tuple-element.68), channel_id=1, source_target_pairs={{0,4},{1,5},{2,6},{3,7},{4,8},{5,9},{6,10},{7,11},{8,12},{9,13},{1... | collective-permute-start | bytes 884744 | tf_op jit(solution)/shard_map/ppermute | solution.py:11
  124.9 40.8 %collective-permute-start.14 = (bf16[192,768]{1,0:T(8,128)(2,1)}, bf16[192,768]{1,0:T(8,128)(2,1)}, u32[]{:S(2)}, u32[]{:S(2)}) collective-permute-start(bf16[192,768]{1,0:T(8,128)(2,1)} %get-tuple-element.70), channel_id=1, source_target_pairs={{0,8},{1,9},{2,10},{3,11},{4,12},{5,13},{6,14},{7,15},{8,0},{9,1},... | collective-permute-start | bytes 884744 | tf_op jit(solution)/shard_map/ppermute | solution.py:11
  128.2 38.0 %collective-permute-start.15 = (bf16[192,768]{1,0:T(8,128)(2,1)}, bf16[192,768]{1,0:T(8,128)(2,1)}, u32[]{:S(2)}, u32[]{:S(2)}) collective-permute-start(bf16[192,768]{1,0:T(8,128)(2,1)} %get-tuple-element.69), channel_id=1, source_target_pairs={{0,12},{1,13},{2,14},{3,15},{4,0},{5,1},{6,2},{7,3},{8,4},{9,5},{1... | collective-permute-start | bytes 884744 | tf_op jit(solution)/shard_map/ppermute | solution.py:11
  131.4 40.7 %collective-permute-start.6 = (bf16[48,3072]{1,0:T(8,128)(2,1)}, bf16[48,3072]{1,0:T(8,128)(2,1)S(1)}, u32[]{:S(2)}, u32[]{:S(2)}) collective-permute-start(bf16[48,3072]{1,0:T(8,128)(2,1)} %get-tuple-element.71), channel_id=1, source_target_pairs={{0,4},{1,5},{2,6},{3,7},{4,8},{5,9},{6,10},{7,11},{8,12},{9,13},{1... | collective-permute-start | bytes 884744 | tf_op jit(solution)/shard_map/ppermute | solution.py:11
  141.2 35.9 %collective-permute-start.7 = (bf16[48,3072]{1,0:T(8,128)(2,1)}, bf16[48,3072]{1,0:T(8,128)(2,1)S(1)}, u32[]{:S(2)}, u32[]{:S(2)}) collective-permute-start(bf16[48,3072]{1,0:T(8,128)(2,1)} %get-tuple-element.73), channel_id=1, source_target_pairs={{0,8},{1,9},{2,10},{3,11},{4,12},{5,13},{6,14},{7,15},{8,0},{9,1},... | collective-permute-start | bytes 884744 | tf_op jit(solution)/shard_map/ppermute | solution.py:11
  146.5 31.5 %collective-permute-start.8 = (bf16[48,3072]{1,0:T(8,128)(2,1)}, bf16[48,3072]{1,0:T(8,128)(2,1)S(1)}, u32[]{:S(2)}, u32[]{:S(2)}) collective-permute-start(bf16[48,3072]{1,0:T(8,128)(2,1)} %get-tuple-element.72), channel_id=1, source_target_pairs={{0,12},{1,13},{2,14},{3,15},{4,0},{5,1},{6,2},{7,3},{8,4},{9,5},{1... | collective-permute-start | bytes 884744 | tf_op jit(solution)/shard_map/ppermute | solution.py:11

commit v2 on v1

--- a/solution.py
+++ b/solution.py
@@ -3,6 +3,8 @@
 import jax
 import jax.numpy as jnp
 from jax import lax
+from jax.experimental import pallas as pl
+from jax.experimental.pallas import tpu as pltpu
 from jax.sharding import PartitionSpec as P
 
 
@@ -30,17 +32,93 @@
     return lax.dynamic_index_in_dim(array, index, axis, keepdims=False)
 
 
-def outer_scatter(partial):
-    outer = partial.shape[0]
+def outer_exchange(rounded):
+    outer = rounded.shape[0]
     count = lax.axis_size("col")
     mine = lax.axis_index("col") // 4
-    rounded = partial.astype(jnp.bfloat16)
-    total = pick(partial, mine, 0)
-    for step in range(1, outer):
-        block = pick(rounded, lax.rem(mine + step, outer), 0)
-        got = permuted(block, lambda i: (i + 4 * step) % count)
-        total = total + got.astype(jnp.float32)
+    return [
+        permuted(pick(rounded, lax.rem(mine + step, outer), 0), lambda i: (i + 4 * step) % count)
+        for step in range(1, outer)
+    ]
+
+
+def outer_total(partial, arrived):
+    total = pick(partial, lax.axis_index("col") // 4, 0)
+    for block in arrived:
+        total = total + block.astype(jnp.float32)
     return total
+
+
+def tail_kernel(
+    dpre_ref, weight_ref, nhat_ref, inverse_ref, gain_ref, scale_ref, views_ref, out_ref, dconv_ref
+):
+    _, rows, wide, channels = views_ref.shape
+    cols = wide - 6
+    dnormed = lax.dot_general(
+        dpre_ref[...],
+        weight_ref[...],
+        (((1,), (1,)), ((), ())),
+        preferred_element_type=jnp.float32,
+    )
+    nhat = nhat_ref[...]
+    out_ref[49:50] = jnp.sum(dnormed * nhat, axis=0, keepdims=True)
+    out_ref[50:51] = scale_ref[...]
+    scaled = dnormed * gain_ref[...]
+    dconv = inverse_ref[...] * (
+        scaled
+        - jnp.mean(scaled, axis=-1, keepdims=True)
+        - nhat * jnp.mean(scaled * nhat, axis=-1, keepdims=True)
+    )
+    dconv_ref[...] = dconv.reshape(dconv_ref.shape)
+
+    def channel_tile(tile, carry):
+        lanes = pl.ds(pl.multiple_of(tile * 128, 128), 128)
+        sums = [[jnp.zeros((cols, 128), jnp.float32) for _ in range(7)] for _ in range(7)]
+        for view in range(2):
+            grads = [dconv_ref[view, row, :, lanes] for row in range(rows)]
+            for source in range(rows):
+                for col_off in range(7):
+                    window = views_ref[view, source, col_off : col_off + cols, lanes]
+                    place = col_off if view == 0 else 6 - col_off
+                    for row_off in range(7):
+                        row = source - row_off + 3
+                        if 0 <= row < rows:
+                            sums[row_off][place] = sums[row_off][place] + window * grads[row]
+        for row_off in range(7):
+            for col_off in range(7):
+                index = row_off * 7 + col_off
+                out_ref[index : index + 1, lanes] = jnp.sum(
+                    sums[row_off][col_off], axis=0, keepdims=True
+                )
+        return carry
+
+    lax.fori_loop(0, channels // 128, channel_tile, 0)
+
+
+def tail(dpre, expand_weight, nhat, inverse, norm_gain, grad_scale, widened):
+    channels = nhat.shape[-1]
+    view_count, rows, wide, _ = widened.shape
+    return pl.pallas_call(
+        tail_kernel,
+        out_shape=jax.ShapeDtypeStruct((51, channels), jnp.float32),
+        scratch_shapes=[pltpu.VMEM((view_count, rows, wide - 6, channels), jnp.float32)],
+        compiler_params=pltpu.CompilerParams(vmem_limit_bytes=32 << 20),
+        cost_estimate=pl.CostEstimate(
+            flops=20_000_000_000, bytes_accessed=30_000_000, transcendentals=0
+        ),
+    )(
+        dpre,
+        expand_weight,
+        nhat.reshape(-1, channels),
+        inverse.reshape(-1, 1),
+        norm_gain[None],
+        grad_scale[None],
+        widened.astype(jnp.float32),
+    )
+
+
+def after(value, *others):
+    return lax.optimization_barrier((value, *others))[0]
 
 
 def all_sum(block):
@@ -87,7 +165,7 @@
     normed = (nhat * norm_gain).astype(jnp.bfloat16).reshape(-1, channels)
     pre = jnp.dot(normed, expand_weight, preferred_element_type=jnp.float32)
     activated, gelu_slope = gelu_parts(pre)
-    hidden = activated.astype(jnp.bfloat16)
+    hidden = lax.reduce_precision(activated, 8, 7).astype(jnp.bfloat16)
     branch = jnp.dot(hidden, reduce_weight, preferred_element_type=jnp.float32)
     outputs = (views.astype(jnp.float32) + layer_scale * branch.reshape(conv.shape)).astype(
         jnp.bfloat16
@@ -118,8 +196,6 @@
     reduce_quad = jnp.dot(
         contrast_quad.reshape(-1, 4 * pixels), dbranch_quad, preferred_element_type=jnp.float32
     ).reshape(outer, hidden_size // count, channels)
-    grad_reduce = outer_scatter(reduce_quad)
-
     dhidden = lax.dot_general(
         dbranch, reduce_weight, (((1,), (1,)), ((), ())), preferred_element_type=jnp.float32
     )
@@ -137,33 +213,26 @@
         rows = pick(normed_pair, which, 1).reshape(-1, 4 * pixels)
         return jnp.dot(rows, dpre_pair, preferred_element_type=jnp.float32)
 
-    sent = permuted(expand_part(1 - side).astype(jnp.bfloat16), other_side)
-    expand_quad = expand_part(side) + sent.astype(jnp.float32)
-    grad_expand = outer_scatter(expand_quad.reshape(outer, channels // count, hidden_size))
-
-    dnormed = lax.dot_general(
-        dpre, expand_weight, (((1,), (1,)), ((), ())), preferred_element_type=jnp.float32
-    ).reshape(conv.shape)
-    grad_gain_local = jnp.sum(dnormed * nhat, axis=(0, 1, 2))
-    scaled = dnormed * norm_gain
-    dconv = inverse * (
-        scaled
-        - jnp.mean(scaled, axis=-1, keepdims=True)
-        - nhat * jnp.mean(scaled * nhat, axis=-1, keepdims=True)
-    )
-    kernel_rows = []
-    for row_off in range(7):
-        kernel_cols = []
-        for col_off in range(7):
-            window = padded[:, row_off : row_off + row_count, col_off : col_off + col_count]
-            kernel_cols.append(jnp.sum(window * dconv, axis=(1, 2)))
-        kernel_rows.append(jnp.stack(kernel_cols, axis=1))
-    view_kernels = jnp.stack(kernel_rows, axis=1)
-    kernel_local = view_kernels[0] + view_kernels[1][:, ::-1]
-    small = jnp.concatenate(
-        [kernel_local.reshape(49, channels), grad_gain_local[None], grad_scale_local[None]], axis=0
-    )
+    leaving = expand_part(1 - side).astype(jnp.bfloat16)
+    arrived = permuted(leaving, other_side)
+    reduce_rounded = reduce_quad.astype(jnp.bfloat16)
+    reduce_arrived = outer_exchange(reduce_rounded)
+    small = tail(
+        after(dpre, leaving, reduce_rounded),
+        expand_weight,
+        nhat,
+        inverse,
+        norm_gain,
+        grad_scale_local,
+        widened,
+    )
+    arrived, small, *reduce_arrived = lax.optimization_barrier((arrived, small, *reduce_arrived))
+    expand_quad = expand_part(side) + arrived.astype(jnp.float32)
+    expand_quad = expand_quad.reshape(outer, channels // count, hidden_size)
+    expand_arrived = outer_exchange(expand_quad.astype(jnp.bfloat16))
+    grad_reduce = outer_total(reduce_quad, reduce_arrived)
     small = all_sum(small)
+    grad_expand = outer_total(expand_quad, expand_arrived)
     return (
         disagreement,
         grad_expand,

time: 180 us -> 131 us (0.73)
  the two profiles are of different devices: /device:TPU:8 before, /device:TPU:0 now
where the time goes in v2:
time: 131 us
  waiting for transfers between devices  52.8 us (40%)
  starting transfers between devices  29.3 us (22%)
  matrix products  17.3 us (13%)
  local copies, waits for them, and re-layouts  12.8 us (10%)
  other arithmetic  12.2 us (9%)
  Pallas kernels  4.94 us (4%)
  between operations  1.34 us (1%)
    ppermute x18, waiting for transfers between devices, permuted(): return lax.ppermute(block, 'col', [(i, target(i)) for i in range(count)])  51 us
    ppermute x18, starting transfers between devices, permuted(): return lax.ppermute(block, 'col', [(i, target(i)) for i in range(count)])  25.4 us
    dot_general x1, matrix products, on_device(): pre = jnp.dot(normed, expand_weight, preferred_element_type=jnp.float32)  5 us
    pallas_call x1, Pallas kernels, tail(): pl.pallas_call(tail_kernel, out_shape=jax.ShapeDtypeStruct((51, channels)...  4.94 us
    unnamed x45, local copies, waits for them, and re-layouts  4.64 us
    add x2, other arithmetic, outer_total(): total = total + block.astype(jnp.float32)  4.08 us
    dot_general x1, matrix products, on_device(): lax.dot_general(dbranch, reduce_weight, (((1,), (1,)), ((), ())), preferr...  3.88 us
    dot_general x2, matrix products, expand_part(): return jnp.dot(rows, dpre_pair, preferred_element_type=jnp.float32)  3.28 us
  transfers between devices with their start and end apart: 20, of which 8 were waited for; matrix products, arithmetic and copies ran while one was open for 19% of the time, Pallas kernels for 4%

profile of v2, /device:TPU:0, one launch (start us, length us, event | category | flops | bytes accessed | tf_op | source)
XLA Modules:
  0.0 130.7 jit_solution(16803196864671266977)
XLA Ops:
  0.6 5.5 %collective-permute-start = (bf16[8,768]{1,0:T(8,128)(2,1)}, bf16[8,768]{1,0:T(8,128)(2,1)S(1)}, u32[]{:S(2)}, u32[]{:S(2)}) collective-permute-start(bf16[8,768]{1,0:T(8,128)(2,1)} %param.8), channel_id=1, source_target_pairs={{0,15},{1,14},{2,13},{3,12},{4,11},{5,10},{6,9},{7,8},{8,7},{9,6},... | collective-permute-start | bytes 36872 | tf_op jit(solution)/shard_map/ppermute | solution.py:13
  6.1 2.3 %rev.7 = f32[7,7,768]{2,1,0:T(8,128)S(1)} reverse(bf16[7,7,768]{2,1,0:T(8,128)(2,1)} %param.9), dimensions={1} | reverse | bytes 225792 | tf_op jit(solution)/shard_map/rev | solution.py:148
  10.5 2.6 %collective-permute-start.1 = (bf16[2,8,3,768]{3,2,1,0:T(4,128)(2,1)S(1)}, bf16[2,8,3,768]{3,2,1,0:T(4,128)(2,1)S(1)}, u32[]{:S(2)}, u32[]{:S(2)}) collective-permute-start(bf16[2,8,3,768]{3,2,1,0:T(4,128)(2,1)S(1)} %get-tuple-element.94), channel_id=1, source_target_pairs={{0,1},{1,2},{2,3},{3,4},{4,5},{5,6},{6,7},{7,8},{8,9},{9,10},{10,1... | collective-permute-start | bytes 221192 | tf_op jit(solution)/shard_map/ppermute | solution.py:26
  14.6 1.7 %collective-permute-done.2 = bf16[2,8,3,768]{3,2,1,0:T(4,128)(2,1)S(1)} collective-permute-done((bf16[2,8,3,768]{3,2,1,0:T(4,128)(2,1)S(1)}, bf16[2,8,3,768]{3,2,1,0:T(4,128)(2,1)S(1)}, u32[]{:S(2)}, u32[]{:S(2)}) %collective-permute-start.2) | collective-permute-done | bytes 73760 | tf_op jit(solution)/shard_map/ppermute | solution.py:27
  16.5 2.9 %fusion.127 = (f32[2,8,8]{2,1,0:T(8,128)S(1)}, f32[2,8,8,768]{3,2,1,0:T(8,128)S(1)}) fusion(f32[2,768]{1,0:T(2,128)S(1)} %get-tuple-element.98, f32[2,768]{1,0:T(2,128)S(1)} %get-tuple-element.102, f32[2,768]{1,0:T(2,128)S(1)} %get-tuple-element.103, f32[2,768]{1,0:T(2,128)S(1)} %get-tuple-element.104, f32[2,768]{1,0:T(2,128)S(1)} %get-tuple-element.105, ...), kind=kLoop, calls=%fused_computation.325 | loop fusion | flops 9633664 | bytes 4233728 | tf_op jit(solution)/shard_map/reduce_sum | solution.py:160
  20.6 5.0 %fusion.126 = (f32[128,3072]{1,0:T(8,128)S(1)}, bf16[128,3072]{1,0:T(8,128)(2,1)S(1)}, f32[128,3072]{1,0:T(8,128)}) fusion(bf16[128,768]{1,0:T(8,128)(2,1)S(1)} %bitcast.201, bf16[768,3072]{1,0:T(8,128)(2,1)} %weight_ref.1), kind=kOutput, calls=%fused_computation.324 | convolution fusion | flops 608698368 | bytes 8847360 | tf_op jit(solution)/shard_map/dot_general | solution.py:166
  27.6 2.8 %collective-permute-start.6 = (bf16[4,2,192,64]{2,3,1,0:T(8,128)(2,1)S(1)}, bf16[4,2,192,64]{2,3,1,0:T(8,128)(2,1)S(1)}, u32[]{:S(2)}, u32[]{:S(2)}) collective-permute-start(bf16[4,2,192,64]{2,3,1,0:T(8,128)(2,1)S(1)} %bitcast.207), channel_id=1, source_target_pairs={{0,1},{1,0},{2,3},{3,2},{4,5},{5,4},{6,7},{7,6},{8,9},{9,8},{10,11... | collective-permute-start | bytes 589832 | tf_op jit(solution)/shard_map/ppermute | solution.py:13
  30.6 3.3 %fusion.131 = f32[128,768]{1,0:T(8,128)S(1)} fusion(bf16[128,3072]{1,0:T(8,128)(2,1)S(1)} %get-tuple-element.21, bf16[3072,768]{1,0:T(8,128)(2,1)} %param.12), kind=kOutput, calls=%fused_computation.328 | convolution fusion | flops 603979776 | bytes 5898240 | tf_op jit(solution)/shard_map/dot_general | solution.py:169
  34.8 3.9 %fusion.11 = (bf16[1,64,3072]{2,1,0:T(8,128)(2,1)S(1)}, bf16[1,64,3072]{2,1,0:T(8,128)(2,1)S(1)}) fusion(f32[128,3072]{1,0:T(8,128)S(1)} %copy-done.2, bf16[64,768]{1,0:T(8,128)(2,1)S(1)} %fusion.115, bf16[3072,768]{1,0:T(8,128)(2,1)} %param.12), kind=kOutput, calls=%fused_computation.69 | convolution fusion | flops 302972928 | bytes 7176192 | tf_op jit(solution)/shard_map/dot_general | solution.py:199
  41.4 1.4 %collective-permute-start.9 = (bf16[128,768]{1,0:T(8,128)(2,1)}, bf16[128,768]{1,0:T(8,128)(2,1)S(1)}, u32[]{:S(2)}, u32[]{:S(2)}) collective-permute-start(bf16[128,768]{1,0:T(8,128)(2,1)} %pad_maximum_fusion.4), channel_id=1, source_target_pairs={{0,2},{1,3},{2,0},{3,1},{4,6},{5,7},{6,4},{7,5},{8,10},{9,11},{10,... | collective-permute-start | bytes 589832 | tf_op jit(solution)/shard_map/ppermute | solution.py:13
  44.4 1.5 %fusion.121 = (bf16[4,1,48,256]{3,2,1,0:T(8,128)(2,1)}, bf16[4,1,48,256]{3,2,1,0:T(8,128)(2,1)S(1)}) fusion(s32[]{:T(128)S(6)} %select_n.55, bf16[4,2,48,128]{3,2,1,0:T(8,128)(2,1)S(1)} %get-tuple-element.93, bf16[4,2,48,128]{3,2,1,0:T(8,128)(2,1)} %collective-permute-done.3, s32[]{:T(128)S(6)} %select_n.54), kind=kLoop, calls=%fused_computation.211 | loop fusion | flops 393216 | bytes 393224 | tf_op jit(solution)/shard_map/concatenate | solution.py:207
  46.1 3.3 %collective-permute-done.9 = bf16[128,768]{1,0:T(8,128)(2,1)S(1)} collective-permute-done((bf16[128,768]{1,0:T(8,128)(2,1)}, bf16[128,768]{1,0:T(8,128)(2,1)S(1)}, u32[]{:S(2)}, u32[]{:S(2)}) %collective-permute-start.9) | collective-permute-done | bytes 196640 | tf_op jit(solution)/shard_map/ppermute | solution.py:13
  49.4 3.3 %collective-permute-done.7 = bf16[4,192,128]{2,1,0:T(8,128)(2,1)S(1)} collective-permute-done((bf16[4,192,128]{2,1,0:T(8,128)(2,1)}, bf16[4,192,128]{2,1,0:T(8,128)(2,1)S(1)}, u32[]{:S(2)}, u32[]{:S(2)}) %collective-permute-start.7) | collective-permute-done | bytes 196640 | tf_op jit(solution)/shard_map/ppermute | solution.py:13
  52.7 1.9 %fusion.130 = (bf16[4,192,768]{2,1,0:T(8,128)(2,1)S(1)}, f32[4,192,768]{2,1,0:T(8,128)}) fusion(bf16[128,768]{1,0:T(8,128)(2,1)S(1)} %collective-permute-done.9, bf16[64,768]{1,0:T(8,128)(2,1)S(1)} %collective-permute-done.8, bf16[64,768]{1,0:T(8,128)(2,1)S(1)} %fusion.115, bf16[4,192,128]{2,1,0:T(8,128)(2,1)S(1)} %collective-permute-done.7, ...), kind=kOutput, calls=%fused_computation.327 | convolution fusion | flops 304545792 | bytes 4325376 | tf_op jit(solution)/shard_map/dot_general | solution.py:196
  54.9 2.8 %collective-permute-start.11 = (bf16[192,768]{1,0:T(8,128)(2,1)S(1)}, bf16[192,768]{1,0:T(8,128)(2,1)S(1)}, u32[]{:S(2)}, u32[]{:S(2)}) collective-permute-start(bf16[192,768]{1,0:T(8,128)(2,1)S(1)} %get-tuple-element.33), channel_id=1, source_target_pairs={{0,8},{1,9},{2,10},{3,11},{4,12},{5,13},{6,14},{7,15},{8,0},{9,1},... | collective-permute-start | bytes 884744 | tf_op jit(solution)/shard_map/ppermute | solution.py:13
  57.8 2.1 %collective-permute-start.12 = (bf16[192,768]{1,0:T(8,128)(2,1)S(1)}, bf16[192,768]{1,0:T(8,128)(2,1)S(1)}, u32[]{:S(2)}, u32[]{:S(2)}) collective-permute-start(bf16[192,768]{1,0:T(8,128)(2,1)S(1)} %get-tuple-element.32), channel_id=1, source_target_pairs={{0,12},{1,13},{2,14},{3,15},{4,0},{5,1},{6,2},{7,3},{8,4},{9,5},{1... | collective-permute-start | bytes 884744 | tf_op jit(solution)/shard_map/ppermute | solution.py:13
  59.8 1.6 %convolution_convert_fusion = bf16[192,3072]{1,0:T(8,128)(2,1)S(1)} fusion(bf16[192,256]{1,0:T(8,128)(2,1)S(1)} %bitcast.209, bf16[128,3072]{1,0:T(8,128)(2,1)} %collective-permute-done.4, bf16[128,3072]{1,0:T(8,128)(2,1)S(1)} %bitcast.187), kind=kOutput, calls=%fused_computation.43 | convolution fusion | flops 305725440 | bytes 2850816 | tf_op jit(solution)/shard_map/dot_general | solution.py:214
  61.5 1.8 %collective-permute-start.5 = (bf16[192,3072]{1,0:T(8,128)(2,1)S(1)}, bf16[192,3072]{1,0:T(8,128)(2,1)S(1)}, u32[]{:S(2)}, u32[]{:S(2)}) collective-permute-start(bf16[192,3072]{1,0:T(8,128)(2,1)S(1)} %convolution_convert_fusion), channel_id=1, source_target_pairs={{0,2},{1,3},{2,0},{3,1},{4,6},{5,7},{6,4},{7,5},{8,10},{9,11},{10,... | collective-permute-start | bytes 3538952 | tf_op jit(solution)/shard_map/ppermute | solution.py:13
  63.3 2.3 %copy-done = bf16[768,3072]{1,0:T(8,128)(2,1)S(1)} copy-done((bf16[768,3072]{1,0:T(8,128)(2,1)S(1)}, bf16[768,3072]{1,0:T(8,128)(2,1)}, u32[]{:S(2)}) %copy-start) | copy-done | bytes 4718616
  65.6 4.9 %shard_map.118 = f32[51,768]{1,0:T(8,128)S(1)} custom-call(bf16[128,3072]{1,0:T(8,128)(2,1)S(1)} %bitcast.188, bf16[768,3072]{1,0:T(8,128)(2,1)S(1)} %copy-done, f32[128,768]{1,0:T(8,128)S(1)} %bitcast.190, f32[128,1]{1,0:T(8,128)S(1)} %rsqrt.20.inverse_ref, f32[1,768]{1,0:T(1,128)S(1)} %broadcast_in_dim.4.gain_ref, f32[1,768]{1,0:T(1,128)S(1)} %broadcast_in_dim.5.scale_ref, ...), custom_call_target="tpu_custom_call" | custom-call | flops 20000000000 | bytes 30000000 | tf_op jit(solution)/shard_map/pallas_call | solution.py:101
  70.5 6.8 %collective-permute-done.11 = bf16[192,768]{1,0:T(8,128)(2,1)S(1)} collective-permute-done((bf16[192,768]{1,0:T(8,128)(2,1)S(1)}, bf16[192,768]{1,0:T(8,128)(2,1)S(1)}, u32[]{:S(2)}, u32[]{:S(2)}) %collective-permute-start.11) | collective-permute-done | bytes 294944 | tf_op jit(solution)/shard_map/ppermute | solution.py:13
  77.4 10.6 %collective-permute-done.5 = bf16[192,3072]{1,0:T(8,128)(2,1)S(1)} collective-permute-done((bf16[192,3072]{1,0:T(8,128)(2,1)S(1)}, bf16[192,3072]{1,0:T(8,128)(2,1)S(1)}, u32[]{:S(2)}, u32[]{:S(2)}) %collective-permute-start.5) | collective-permute-done | bytes 1179680 | tf_op jit(solution)/shard_map/ppermute | solution.py:13
  88.0 1.7 %convolution_add_fusion = f32[192,3072]{1,0:T(8,128)S(1)} fusion(bf16[192,256]{1,0:T(8,128)(2,1)S(1)} %bitcast.206, bf16[192,3072]{1,0:T(8,128)(2,1)S(1)} %collective-permute-done.5, bf16[128,3072]{1,0:T(8,128)(2,1)} %collective-permute-done.4, bf16[128,3072]{1,0:T(8,128)(2,1)S(1)} %bitcast.189), kind=kOutput, calls=%fused_computation.42 | convolution fusion | flops 306315264 | bytes 5210112 | tf_op jit(solution)/shard_map/dot_general | solution.py:214
  89.9 1.3 %copy-done.1 = f32[192,3072]{1,0:T(8,128)} copy-done((f32[192,3072]{1,0:T(8,128)}, f32[192,3072]{1,0:T(8,128)S(1)}, u32[]{:S(2)}) %copy-start.1) | copy-done | bytes 2359320
  91.2 1.5 %collective-permute-start.17 = (f32[51,768]{1,0:T(8,128)S(1)}, f32[51,768]{1,0:T(8,128)S(1)}, u32[]{:S(2)}, u32[]{:S(2)}) collective-permute-start(f32[51,768]{1,0:T(8,128)S(1)} %add.354), channel_id=1, source_target_pairs={{0,2},{1,3},{2,0},{3,1},{4,6},{5,7},{6,4},{7,5},{8,10},{9,11},{10,... | collective-permute-start | bytes 470024 | tf_op jit(solution)/shard_map/ppermute | solution.py:13
  93.7 3.0 %collective-permute-start.15 = (bf16[48,3072]{1,0:T(8,128)(2,1)S(1)}, bf16[48,3072]{1,0:T(8,128)(2,1)S(1)}, u32[]{:S(2)}, u32[]{:S(2)}) collective-permute-start(bf16[48,3072]{1,0:T(8,128)(2,1)S(1)} %get-tuple-element.30), channel_id=1, source_target_pairs={{0,12},{1,13},{2,14},{3,15},{4,0},{5,1},{6,2},{7,3},{8,4},{9,5},{1... | collective-permute-start | bytes 884744 | tf_op jit(solution)/shard_map/ppermute | solution.py:13
  96.6 1.4 %collective-permute-done.17 = f32[51,768]{1,0:T(8,128)S(1)} collective-permute-done((f32[51,768]{1,0:T(8,128)S(1)}, f32[51,768]{1,0:T(8,128)S(1)}, u32[]{:S(2)}, u32[]{:S(2)}) %collective-permute-start.17) | collective-permute-done | bytes 156704 | tf_op jit(solution)/shard_map/ppermute | solution.py:13
  98.2 2.0 %fusion.8 = f32[192,768]{1,0:T(8,128)} fusion(bf16[192,768]{1,0:T(8,128)(2,1)S(1)} %collective-permute-done.12, bf16[192,768]{1,0:T(8,128)(2,1)S(1)} %collective-permute-done.11, bf16[192,768]{1,0:T(8,128)(2,1)S(1)} %collective-permute-done.10, f32[4,192,768]{2,1,0:T(8,128)} %get-tuple-element.97, s32[]{:T(128)S(6)} %select_n.60), kind=kLoop, calls=%fused_computation.65 | loop fusion | flops 884736 | bytes 2064388 | tf_op jit(solution)/shard_map/add | solution.py:48
  100.2 19.0 %collective-permute-done.18 = f32[51,768]{1,0:T(8,128)S(1)} collective-permute-done((f32[51,768]{1,0:T(8,128)S(1)}, f32[51,768]{1,0:T(8,128)S(1)}, u32[]{:S(2)}, u32[]{:S(2)}) %collective-permute-start.18) | collective-permute-done | bytes 156704 | tf_op jit(solution)/shard_map/ppermute | solution.py:13
  119.3 1.5 %collective-permute-start.19 = (f32[51,768]{1,0:T(8,128)S(1)}, f32[51,768]{1,0:T(8,128)S(1)}, u32[]{:S(2)}, u32[]{:S(2)}) collective-permute-start(f32[51,768]{1,0:T(8,128)S(1)} %add.356), channel_id=1, source_target_pairs={{0,8},{1,9},{2,10},{3,11},{4,12},{5,13},{6,14},{7,15},{8,0},{9,1},... | collective-permute-start | bytes 470024 | tf_op jit(solution)/shard_map/ppermute | solution.py:13
  120.8 2.0 %fusion.10 = f32[48,3072]{1,0:T(8,128)} fusion(bf16[48,3072]{1,0:T(8,128)(2,1)S(1)} %collective-permute-done.15, bf16[48,3072]{1,0:T(8,128)(2,1)S(1)} %collective-permute-done.14, bf16[48,3072]{1,0:T(8,128)(2,1)S(1)} %collective-permute-done.13, f32[4,48,3072]{2,1,0:T(8,128)} %bitcast.192, s32[]{:T(128)S(6)} %select_n.60), kind=kLoop, calls=%fused_computation.68 | loop fusion | flops 884736 | bytes 2064388 | tf_op jit(solution)/shard_map/add | solution.py:48
  122.9 6.5 %collective-permute-done.19 = f32[51,768]{1,0:T(8,128)S(1)} collective-permute-done((f32[51,768]{1,0:T(8,128)S(1)}, f32[51,768]{1,0:T(8,128)S(1)}, u32[]{:S(2)}, u32[]{:S(2)}) %collective-permute-start.19) | collective-permute-done | bytes 156704 | tf_op jit(solution)/shard_map/ppermute | solution.py:13
  (108 shorter events, 14.9 us)
Async XLA Ops:
  0.6 9.6 %collective-permute-start = (bf16[8,768]{1,0:T(8,128)(2,1)}, bf16[8,768]{1,0:T(8,128)(2,1)S(1)}, u32[]{:S(2)}, u32[]{:S(2)}) collective-permute-start(bf16[8,768]{1,0:T(8,128)(2,1)} %param.8), channel_id=1, source_target_pairs={{0,15},{1,14},{2,13},{3,12},{4,11},{5,10},{6,9},{7,8},{8,7},{9,6},... | collective-permute-start | bytes 36872 | tf_op jit(solution)/shard_map/ppermute | solution.py:13
  9.3 0.9 copy-start.4
  9.3 1.1 copy-start.8
  9.5 5.0 %copy-start.7 = (f32[768]{0:T(1024)S(1)}, f32[768]{0:T(1024)}, u32[]{:S(2)}) copy-start(f32[768]{0:T(1024)} %param.10) | copy-start | bytes 9220
  10.5 4.0 %collective-permute-start.1 = (bf16[2,8,3,768]{3,2,1,0:T(4,128)(2,1)S(1)}, bf16[2,8,3,768]{3,2,1,0:T(4,128)(2,1)S(1)}, u32[]{:S(2)}, u32[]{:S(2)}) collective-permute-start(bf16[2,8,3,768]{3,2,1,0:T(4,128)(2,1)S(1)} %get-tuple-element.94), channel_id=1, source_target_pairs={{0,1},{1,2},{2,3},{3,4},{4,5},{5,6},{6,7},{7,8},{8,9},{9,10},{10,1... | collective-permute-start | bytes 221192 | tf_op jit(solution)/shard_map/ppermute | solution.py:26
  13.1 3.2 %collective-permute-start.2 = (bf16[2,8,3,768]{3,2,1,0:T(4,128)(2,1)S(1)}, bf16[2,8,3,768]{3,2,1,0:T(4,128)(2,1)S(1)}, u32[]{:S(2)}, u32[]{:S(2)}) collective-permute-start(bf16[2,8,3,768]{3,2,1,0:T(4,128)(2,1)S(1)} %get-tuple-element.95), channel_id=1, source_target_pairs={{1,0},{2,1},{3,2},{4,3},{5,4},{6,5},{7,6},{8,7},{9,8},{10,9},{11,1... | collective-permute-start | bytes 221192 | tf_op jit(solution)/shard_map/ppermute | solution.py:27
  27.6 15.2 %collective-permute-start.6 = (bf16[4,2,192,64]{2,3,1,0:T(8,128)(2,1)S(1)}, bf16[4,2,192,64]{2,3,1,0:T(8,128)(2,1)S(1)}, u32[]{:S(2)}, u32[]{:S(2)}) collective-permute-start(bf16[4,2,192,64]{2,3,1,0:T(8,128)(2,1)S(1)} %bitcast.207), channel_id=1, source_target_pairs={{0,1},{1,0},{2,3},{3,2},{4,5},{5,4},{6,7},{7,6},{8,9},{9,8},{10,11... | collective-permute-start | bytes 589832 | tf_op jit(solution)/shard_map/ppermute | solution.py:13
  30.6 3.3 %copy-start.6 = (f32[768]{0:T(1024)S(1)}, f32[768]{0:T(1024)}, u32[]{:S(2)}) copy-start(f32[768]{0:T(1024)} %param.13) | copy-start | bytes 9220
  30.6 4.1 %copy-start.2 = (f32[128,3072]{1,0:T(8,128)S(1)}, f32[128,3072]{1,0:T(8,128)}, u32[]{:S(2)}) copy-start(f32[128,3072]{1,0:T(8,128)} %get-tuple-element.28) | copy-start | bytes 4718596
  34.7 6.0 %collective-permute-start.8 = (bf16[64,768]{1,0:T(8,128)(2,1)S(1)}, bf16[64,768]{1,0:T(8,128)(2,1)S(1)}, u32[]{:S(2)}, u32[]{:S(2)}) collective-permute-start(bf16[64,768]{1,0:T(8,128)(2,1)S(1)} %fusion.115), channel_id=1, source_target_pairs={{0,1},{1,0},{2,3},{3,2},{4,5},{5,4},{6,7},{7,6},{8,9},{9,8},{10,11... | collective-permute-start | bytes 294920 | tf_op jit(solution)/shard_map/ppermute | solution.py:13
  38.6 0.9 copy-start.3
  38.7 21.1 %collective-permute-start.4 = (bf16[128,3072]{1,0:T(8,128)(2,1)S(1)}, bf16[128,3072]{1,0:T(8,128)(2,1)}, u32[]{:S(2)}, u32[]{:S(2)}) collective-permute-start(bf16[128,3072]{1,0:T(8,128)(2,1)S(1)} %bitcast.186), channel_id=1, source_target_pairs={{0,1},{1,0},{2,3},{3,2},{4,5},{5,4},{6,7},{7,6},{8,9},{9,8},{10,11... | collective-permute-start | bytes 2359304 | tf_op jit(solution)/shard_map/ppermute | solution.py:13
  40.2 4.2 %collective-permute-start.3 = (bf16[4,2,48,128]{3,2,1,0:T(8,128)(2,1)}, bf16[4,2,48,128]{3,2,1,0:T(8,128)(2,1)}, u32[]{:S(2)}, u32[]{:S(2)}) collective-permute-start(bf16[4,2,48,128]{3,2,1,0:T(8,128)(2,1)} %get-tuple-element.92), channel_id=1, source_target_pairs={{0,1},{1,0},{2,3},{3,2},{4,5},{5,4},{6,7},{7,6},{8,9},{9,8},{10,11... | collective-permute-start | bytes 294920 | tf_op jit(solution)/shard_map/ppermute | solution.py:13
  41.4 8.0 %collective-permute-start.9 = (bf16[128,768]{1,0:T(8,128)(2,1)}, bf16[128,768]{1,0:T(8,128)(2,1)S(1)}, u32[]{:S(2)}, u32[]{:S(2)}) collective-permute-start(bf16[128,768]{1,0:T(8,128)(2,1)} %pad_maximum_fusion.4), channel_id=1, source_target_pairs={{0,2},{1,3},{2,0},{3,1},{4,6},{5,7},{6,4},{7,5},{8,10},{9,11},{10,... | collective-permute-start | bytes 589832 | tf_op jit(solution)/shard_map/ppermute | solution.py:13
  43.8 8.9 %collective-permute-start.7 = (bf16[4,192,128]{2,1,0:T(8,128)(2,1)}, bf16[4,192,128]{2,1,0:T(8,128)(2,1)S(1)}, u32[]{:S(2)}, u32[]{:S(2)}) collective-permute-start(bf16[4,192,128]{2,1,0:T(8,128)(2,1)} %bitcast.208), channel_id=1, source_target_pairs={{0,2},{1,3},{2,0},{3,1},{4,6},{5,7},{6,4},{7,5},{8,10},{9,11},{10,... | collective-permute-start | bytes 589832 | tf_op jit(solution)/shard_map/ppermute | solution.py:13
  54.5 5.3 %copy-start.5 = (bf16[4,1,48,256]{3,2,1,0:T(8,128)(2,1)S(1)}, bf16[4,1,48,256]{3,2,1,0:T(8,128)(2,1)}, u32[]{:S(2)}) copy-start(bf16[4,1,48,256]{3,2,1,0:T(8,128)(2,1)} %get-tuple-element.90) | copy-start | bytes 294916
  54.6 15.9 %collective-permute-start.10 = (bf16[192,768]{1,0:T(8,128)(2,1)S(1)}, bf16[192,768]{1,0:T(8,128)(2,1)S(1)}, u32[]{:S(2)}, u32[]{:S(2)}) collective-permute-start(bf16[192,768]{1,0:T(8,128)(2,1)S(1)} %get-tuple-element.34), channel_id=1, source_target_pairs={{0,4},{1,5},{2,6},{3,7},{4,8},{5,9},{6,10},{7,11},{8,12},{9,13},{1... | collective-permute-start | bytes 884744 | tf_op jit(solution)/shard_map/ppermute | solution.py:13
  54.9 22.5 %collective-permute-start.11 = (bf16[192,768]{1,0:T(8,128)(2,1)S(1)}, bf16[192,768]{1,0:T(8,128)(2,1)S(1)}, u32[]{:S(2)}, u32[]{:S(2)}) collective-permute-start(bf16[192,768]{1,0:T(8,128)(2,1)S(1)} %get-tuple-element.33), channel_id=1, source_target_pairs={{0,8},{1,9},{2,10},{3,11},{4,12},{5,13},{6,14},{7,15},{8,0},{9,1},... | collective-permute-start | bytes 884744 | tf_op jit(solution)/shard_map/ppermute | solution.py:13
  57.8 19.6 %collective-permute-start.12 = (bf16[192,768]{1,0:T(8,128)(2,1)S(1)}, bf16[192,768]{1,0:T(8,128)(2,1)S(1)}, u32[]{:S(2)}, u32[]{:S(2)}) collective-permute-start(bf16[192,768]{1,0:T(8,128)(2,1)S(1)} %get-tuple-element.32), channel_id=1, source_target_pairs={{0,12},{1,13},{2,14},{3,15},{4,0},{5,1},{6,2},{7,3},{8,4},{9,5},{1... | collective-permute-start | bytes 884744 | tf_op jit(solution)/shard_map/ppermute | solution.py:13
  61.5 26.6 %collective-permute-start.5 = (bf16[192,3072]{1,0:T(8,128)(2,1)S(1)}, bf16[192,3072]{1,0:T(8,128)(2,1)S(1)}, u32[]{:S(2)}, u32[]{:S(2)}) collective-permute-start(bf16[192,3072]{1,0:T(8,128)(2,1)S(1)} %convolution_convert_fusion), channel_id=1, source_target_pairs={{0,2},{1,3},{2,0},{3,1},{4,6},{5,7},{6,4},{7,5},{8,10},{9,11},{10,... | collective-permute-start | bytes 3538952 | tf_op jit(solution)/shard_map/ppermute | solution.py:13
  63.3 2.3 %copy-start = (bf16[768,3072]{1,0:T(8,128)(2,1)S(1)}, bf16[768,3072]{1,0:T(8,128)(2,1)}, u32[]{:S(2)}) copy-start(bf16[768,3072]{1,0:T(8,128)(2,1)} %weight_ref.1) | copy-start | bytes 14155780
  88.0 3.2 %collective-permute-start.16 = (f32[51,768]{1,0:T(8,128)S(1)}, f32[51,768]{1,0:T(8,128)S(1)}, u32[]{:S(2)}, u32[]{:S(2)}) collective-permute-start(f32[51,768]{1,0:T(8,128)S(1)} %shard_map.118), channel_id=1, source_target_pairs={{0,1},{1,0},{2,3},{3,2},{4,5},{5,4},{6,7},{7,6},{8,9},{9,8},{10,11... | collective-permute-start | bytes 470024 | tf_op jit(solution)/shard_map/ppermute | solution.py:13
  89.7 1.5 %copy-start.1 = (f32[192,3072]{1,0:T(8,128)}, f32[192,3072]{1,0:T(8,128)S(1)}, u32[]{:S(2)}) copy-start(f32[192,3072]{1,0:T(8,128)S(1)} %convolution_add_fusion) | copy-start | bytes 7077892
  91.2 6.9 %collective-permute-start.17 = (f32[51,768]{1,0:T(8,128)S(1)}, f32[51,768]{1,0:T(8,128)S(1)}, u32[]{:S(2)}, u32[]{:S(2)}) collective-permute-start(f32[51,768]{1,0:T(8,128)S(1)} %add.354), channel_id=1, source_target_pairs={{0,2},{1,3},{2,0},{3,1},{4,6},{5,7},{6,4},{7,5},{8,10},{9,11},{10,... | collective-permute-start | bytes 470024 | tf_op jit(solution)/shard_map/ppermute | solution.py:13
  92.8 28.1 %collective-permute-start.13 = (bf16[48,3072]{1,0:T(8,128)(2,1)S(1)}, bf16[48,3072]{1,0:T(8,128)(2,1)S(1)}, u32[]{:S(2)}, u32[]{:S(2)}) collective-permute-start(bf16[48,3072]{1,0:T(8,128)(2,1)S(1)} %get-tuple-element.29), channel_id=1, source_target_pairs={{0,4},{1,5},{2,6},{3,7},{4,8},{5,9},{6,10},{7,11},{8,12},{9,13},{1... | collective-permute-start | bytes 884744 | tf_op jit(solution)/shard_map/ppermute | solution.py:13
  92.8 28.0 %collective-permute-start.14 = (bf16[48,3072]{1,0:T(8,128)(2,1)S(1)}, bf16[48,3072]{1,0:T(8,128)(2,1)S(1)}, u32[]{:S(2)}, u32[]{:S(2)}) collective-permute-start(bf16[48,3072]{1,0:T(8,128)(2,1)S(1)} %get-tuple-element.31), channel_id=1, source_target_pairs={{0,8},{1,9},{2,10},{3,11},{4,12},{5,13},{6,14},{7,15},{8,0},{9,1},... | collective-permute-start | bytes 884744 | tf_op jit(solution)/shard_map/ppermute | solution.py:13
  93.7 27.2 %collective-permute-start.15 = (bf16[48,3072]{1,0:T(8,128)(2,1)S(1)}, bf16[48,3072]{1,0:T(8,128)(2,1)S(1)}, u32[]{:S(2)}, u32[]{:S(2)}) collective-permute-start(bf16[48,3072]{1,0:T(8,128)(2,1)S(1)} %get-tuple-element.30), channel_id=1, source_target_pairs={{0,12},{1,13},{2,14},{3,15},{4,0},{5,1},{6,2},{7,3},{8,4},{9,5},{1... | collective-permute-start | bytes 884744 | tf_op jit(solution)/shard_map/ppermute | solution.py:13
  98.1 21.2 %collective-permute-start.18 = (f32[51,768]{1,0:T(8,128)S(1)}, f32[51,768]{1,0:T(8,128)S(1)}, u32[]{:S(2)}, u32[]{:S(2)}) collective-permute-start(f32[51,768]{1,0:T(8,128)S(1)} %add.355), channel_id=1, source_target_pairs={{0,4},{1,5},{2,6},{3,7},{4,0},{5,1},{6,2},{7,3},{8,12},{9,13},{10,... | collective-permute-start | bytes 470024 | tf_op jit(solution)/shard_map/ppermute | solution.py:13
  119.3 10.0 %collective-permute-start.19 = (f32[51,768]{1,0:T(8,128)S(1)}, f32[51,768]{1,0:T(8,128)S(1)}, u32[]{:S(2)}, u32[]{:S(2)}) collective-permute-start(f32[51,768]{1,0:T(8,128)S(1)} %add.356), channel_id=1, source_target_pairs={{0,8},{1,9},{2,10},{3,11},{4,12},{5,13},{6,14},{7,15},{8,0},{9,1},... | collective-permute-start | bytes 470024 | tf_op jit(solution)/shard_map/ppermute | solution.py:13

commit v3 on v2

--- a/solution.py
+++ b/solution.py
@@ -19,13 +19,22 @@
     return (pre * normal_cdf, normal_cdf + pre * density)
 
 
-def with_halo(block, width):
-    count = lax.axis_size("col")
-    forward = [(i, i + 1) for i in range(count - 1)]
-    backward = [(target, source) for source, target in forward]
-    low = lax.ppermute(block[:, :, -width:], "col", forward)
-    high = lax.ppermute(block[:, :, :width], "col", backward)
-    return jnp.concatenate([low, block, high], axis=2)
+def shifted(block, step):
+    count = lax.axis_size("col")
+    return lax.ppermute(
+        block, "col", [(i, i + step) for i in range(count) if 0 <= i + step < count]
+    )
+
+
+def reflected(block, last):
+    count = lax.axis_size("col")
+    return lax.ppermute(
+        block, "col", [(i, last - i) for i in range(count) if 0 <= last - i < count]
+    )
+
+
+def rounded_f32(value):
+    return lax.reduce_precision(value, 8, 7)
 
 
 def pick(array, index, axis):
@@ -63,6 +72,7 @@
     nhat = nhat_ref[...]
     out_ref[49:50] = jnp.sum(dnormed * nhat, axis=0, keepdims=True)
     out_ref[50:51] = scale_ref[...]
+    out_ref[51:64] = jnp.zeros((13, channels), jnp.float32)
     scaled = dnormed * gain_ref[...]
     dconv = inverse_ref[...] * (
         scaled
@@ -100,7 +110,7 @@
     view_count, rows, wide, _ = widened.shape
     return pl.pallas_call(
         tail_kernel,
-        out_shape=jax.ShapeDtypeStruct((51, channels), jnp.float32),
+        out_shape=jax.ShapeDtypeStruct((64, channels), jnp.float32),
         scratch_shapes=[pltpu.VMEM((view_count, rows, wide - 6, channels), jnp.float32)],
         compiler_params=pltpu.CompilerParams(vmem_limit_bytes=32 << 20),
         cost_estimate=pl.CostEstimate(
@@ -113,19 +123,12 @@
         inverse.reshape(-1, 1),
         norm_gain[None],
         grad_scale[None],
-        widened.astype(jnp.float32),
+        widened,
     )
 
 
 def after(value, *others):
     return lax.optimization_barrier((value, *others))[0]
-
-
-def all_sum(block):
-    count = lax.axis_size("col")
-    for bit in range(count.bit_length() - 1):
-        block = block + permuted(block, lambda i: i ^ (1 << bit))
-    return block
 
 
 def on_device(
@@ -141,13 +144,23 @@
     hidden_size = expand_weight.shape[1]
     pixels = row_count * col_count
 
-    mirrored_table = permuted(column_table, lambda i: count - 1 - i)[::-1]
-    tables = jnp.stack([column_table, mirrored_table]).astype(jnp.float32)
-    views = (features.astype(jnp.float32)[None] + tables[:, None]).astype(jnp.bfloat16)
+    edge = jnp.concatenate([features, column_table[None]], axis=0)
+    low = shifted(edge[:, -3:], 1)
+    high = shifted(edge[:, :3], -1)
+    mirror = reflected(column_table, count - 1)
+    mirror_low = reflected(column_table[:3], count)
+    mirror_high = reflected(column_table[-3:], count - 2)
+    wide = jnp.concatenate([low, edge, high], axis=1).astype(jnp.float32)
+    mirror_wide = jnp.concatenate([mirror_high, mirror, mirror_low], axis=0).astype(jnp.float32)
+    mirror_wide = jnp.concatenate(
+        [mirror_wide[i : i + 1] for i in reversed(range(col_count + 6))], axis=0
+    )
+    tables = jnp.stack([wide[-1], mirror_wide])
+    widened = rounded_f32(wide[None, :-1] + tables[:, None])
+    views = widened[:, :, 3:-3]
     kernel_f = dw_kernel.astype(jnp.float32)
     kernels = jnp.stack([kernel_f, kernel_f[:, ::-1]])
-    widened = with_halo(views, 3)
-    padded = jnp.pad(widened.astype(jnp.float32), ((0, 0), (3, 3), (0, 0), (0, 0)))
+    padded = jnp.pad(widened, ((0, 0), (3, 3), (0, 0), (0, 0)))
     conv = jnp.zeros((2, row_count, col_count, channels), jnp.float32)
     for row_off in range(7):
         for col_off in range(7):
@@ -165,12 +178,24 @@
     normed = (nhat * norm_gain).astype(jnp.bfloat16).reshape(-1, channels)
     pre = jnp.dot(normed, expand_weight, preferred_element_type=jnp.float32)
     activated, gelu_slope = gelu_parts(pre)
-    hidden = lax.reduce_precision(activated, 8, 7).astype(jnp.bfloat16)
+    hidden = rounded_f32(activated).astype(jnp.bfloat16)
+    hiddens = hidden.astype(jnp.float32).reshape(2, pixels, hidden_size)
+    contrast = (hiddens[0] - hiddens[1]).astype(jnp.bfloat16)
+    contrast_t = contrast.T.reshape(outer, 2, 2, hidden_size // count, pixels)
+    other_core = lambda i: i ^ 1
+    other_side = lambda i: i ^ 2
+    mates = [(0, 0), (0, 1), (1, 0), (1, 1)]
+    contrast_parts = []
+    for side_step, core_step in mates:
+        part = pick(
+            pick(contrast_t, lax.rem(core + core_step, 2), 2), lax.rem(side + side_step, 2), 1
+        )
+        hop = 2 * side_step + core_step
+        contrast_parts.append(permuted(part, lambda i: i ^ hop) if hop else part)
     branch = jnp.dot(hidden, reduce_weight, preferred_element_type=jnp.float32)
-    outputs = (views.astype(jnp.float32) + layer_scale * branch.reshape(conv.shape)).astype(
-        jnp.bfloat16
-    )
-    difference = outputs[0].astype(jnp.float32) - outputs[1].astype(jnp.float32)
+    branch, contrast_parts = lax.optimization_barrier((branch, contrast_parts))
+    outputs = rounded_f32(views + layer_scale * branch.reshape(conv.shape))
+    difference = outputs[0] - outputs[1]
     disagreement = difference.astype(jnp.bfloat16)
     residual = (difference * (1.0 / math.sqrt(row_count * total_cols))).astype(jnp.bfloat16)
     residual = lax.optimization_barrier(residual)
@@ -179,30 +204,20 @@
     grad_scale_local = jnp.sum((branches[0] - branches[1]) * flat_grad, axis=0)
     dbranch = (layer_scale * flat_grad).astype(jnp.bfloat16)
 
-    hiddens = hidden.astype(jnp.float32).reshape(2, pixels, hidden_size)
-    contrast = (hiddens[0] - hiddens[1]).astype(jnp.bfloat16)
-    contrast_t = contrast.T.reshape(outer, 2, 2, hidden_size // count, pixels)
-    other_core = lambda i: i ^ 1
-    other_side = lambda i: i ^ 2
-    contrast_pair = jnp.concatenate(
-        [pick(contrast_t, core, 2), permuted(pick(contrast_t, 1 - core, 2), other_core)], axis=-1
-    )
-    dbranch_pair = jnp.concatenate([dbranch, permuted(dbranch, other_core)], axis=0)
-    contrast_quad = jnp.concatenate(
-        [pick(contrast_pair, side, 1), permuted(pick(contrast_pair, 1 - side, 1), other_side)],
-        axis=-1,
-    )
-    dbranch_quad = jnp.concatenate([dbranch_pair, permuted(dbranch_pair, other_side)], axis=0)
+    dbranch_parts = [dbranch] + [permuted(dbranch, lambda i: i ^ hop) for hop in range(1, 4)]
+    dhidden = lax.dot_general(
+        dbranch, reduce_weight, (((1,), (1,)), ((), ())), preferred_element_type=jnp.float32
+    )
+    slopes = gelu_slope.reshape(2, pixels, hidden_size)
+    dpre = jnp.stack([dhidden * slopes[0], -dhidden * slopes[1]]).astype(jnp.bfloat16)
+    dpre = dpre.reshape(2 * pixels, hidden_size)
+
+    dpre, dbranch_parts = lax.optimization_barrier((dpre, dbranch_parts))
+    contrast_quad = jnp.concatenate(contrast_parts, axis=-1)
+    dbranch_quad = jnp.concatenate(dbranch_parts, axis=0)
     reduce_quad = jnp.dot(
         contrast_quad.reshape(-1, 4 * pixels), dbranch_quad, preferred_element_type=jnp.float32
     ).reshape(outer, hidden_size // count, channels)
-    dhidden = lax.dot_general(
-        dbranch, reduce_weight, (((1,), (1,)), ((), ())), preferred_element_type=jnp.float32
-    )
-    slopes = gelu_slope.reshape(2, pixels, hidden_size)
-    dpre = jnp.stack([dhidden * slopes[0], -dhidden * slopes[1]]).astype(jnp.bfloat16)
-    dpre = dpre.reshape(2 * pixels, hidden_size)
-
     normed_t = normed.T.reshape(outer, 2, 2, channels // count, 2 * pixels)
     normed_pair = jnp.concatenate(
         [pick(normed_t, core, 2), permuted(pick(normed_t, 1 - core, 2), other_core)], axis=-1
@@ -226,12 +241,21 @@
         grad_scale_local,
         widened,
     )
-    arrived, small, *reduce_arrived = lax.optimization_barrier((arrived, small, *reduce_arrived))
+    small, reduce_arrived = lax.optimization_barrier((small, reduce_arrived))
+    halves = small.reshape(2, -1, channels)
+    half = pick(halves, core, 0) + permuted(pick(halves, 1 - core, 0), other_core)
+    for bit in range(2, count.bit_length() - 1):
+        half = half + permuted(half, lambda i: i ^ (1 << bit))
+    arrived, half = lax.optimization_barrier((arrived, half))
     expand_quad = expand_part(side) + arrived.astype(jnp.float32)
     expand_quad = expand_quad.reshape(outer, channels // count, hidden_size)
     expand_arrived = outer_exchange(expand_quad.astype(jnp.bfloat16))
     grad_reduce = outer_total(reduce_quad, reduce_arrived)
-    small = all_sum(small)
+    half = half + permuted(half, other_side)
+    other_half = permuted(half, other_core)
+    small = jnp.concatenate(
+        [jnp.where(core == 0, half, other_half), jnp.where(core == 0, other_half, half)], axis=0
+    )
     grad_expand = outer_total(expand_quad, expand_arrived)
     return (
         disagreement,

time: 131 us -> 147 us (1.12)
  waiting for transfers between devices: 52.8 us -> 61.3 us
  local copies, waits for them, and re-layouts: 12.8 us -> 16.9 us
  matrix products: 17.3 us -> 18.8 us
    ppermute x2 -> x5, starting transfers between devices: 3.88 us -> 13.2 us  [the longest x3 8.61 us: reflected(): lax.ppermute(block, 'col', [(i, last - i) for i in range(count) if 0 <= l...]
    ppermute x18 -> x20, waiting for transfers between devices: 51 us -> 59.6 us  [permuted(): return lax.ppermute(block, 'col', [(i, target(i)) for i in range(count)])]
    ppermute x18 -> x20, starting transfers between devices: 25.4 us -> 16.9 us  [permuted(): return lax.ppermute(block, 'col', [(i, target(i)) for i in range(count)])]
    dynamic_slice x3 -> x5, local copies, waits for them, and re-layouts: 2.07 us -> 8.5 us  [pick(): return lax.dynamic_index_in_dim(array, index, axis, keepdims=False)]
    unnamed x45 -> x48, local copies, waits for them, and re-layouts: 4.64 us -> 0.31 us
  transfers between devices with their start and end apart: 20 -> 25, of which waited for: 8 -> 12; matrix products, arithmetic and copies ran while one was open for 19% -> 29% of each run, Pallas kernels for 4% -> 3%
where the time goes in v3:
time: 147 us; the launch traced here: 146 us
  waiting for transfers between devices  61.3 us (42%)
  starting transfers between devices  30.1 us (20%)
  matrix products  18.8 us (13%)
  local copies, waits for them, and re-layouts  16.9 us (11%)
  other arithmetic  12.4 us (8%)
  Pallas kernels  4.94 us (3%)
  between operations  1.51 us (1%)
    ppermute x20, waiting for transfers between devices, permuted(): return lax.ppermute(block, 'col', [(i, target(i)) for i in range(count)])  59.6 us
    ppermute x20, starting transfers between devices, permuted(): return lax.ppermute(block, 'col', [(i, target(i)) for i in range(count)])  16.9 us
    ppermute x3, starting transfers between devices, reflected(): lax.ppermute(block, 'col', [(i, last - i) for i in range(count) if 0 <= l...  8.61 us
    dynamic_slice x5, local copies, waits for them, and re-layouts, pick(): return lax.dynamic_index_in_dim(array, index, axis, keepdims=False)  8.5 us
    pallas_call x1, Pallas kernels, tail(): pl.pallas_call(tail_kernel, out_shape=jax.ShapeDtypeStruct((64, channels)...  4.94 us
    dot_general x1, matrix products, on_device(): pre = jnp.dot(normed, expand_weight, preferred_element_type=jnp.float32)  4.75 us
    ppermute x2, starting transfers between devices, shifted(): lax.ppermute(block, 'col', [(i, i + step) for i in range(count) if 0 <= i...  4.58 us
    dot_general x1, matrix products, on_device(): lax.dot_general(dbranch, reduce_weight, (((1,), (1,)), ((), ())), preferr...  3.87 us
  transfers between devices with their start and end apart: 25, of which 12 were waited for; matrix products, arithmetic and copies ran while one was open for 29% of the time, Pallas kernels for 3%

profile of v3, /device:TPU:0, one launch (start us, length us, event | category | flops | bytes accessed | tf_op | source)
XLA Modules:
  0.0 145.9 jit_solution(3111152018136147457)
XLA Ops:
  0.6 5.5 %collective-permute-start.3 = (bf16[8,768]{1,0:T(8,128)(2,1)}, bf16[8,768]{1,0:T(8,128)(2,1)S(1)}, u32[]{:S(2)}, u32[]{:S(2)}) collective-permute-start(bf16[8,768]{1,0:T(8,128)(2,1)} %param.8), channel_id=1, source_target_pairs={{0,15},{1,14},{2,13},{3,12},{4,11},{5,10},{6,9},{7,8},{8,7},{9,6},... | collective-permute-start | bytes 36872 | tf_op jit(solution)/shard_map/ppermute | solution.py:31
  6.9 2.5 %collective-permute-start.2 = (bf16[3,768]{1,0:T(4,128)(2,1)S(1)}, bf16[3,768]{1,0:T(4,128)(2,1)S(1)}, u32[]{:S(2)}, u32[]{:S(2)}) collective-permute-start(bf16[3,768]{1,0:T(4,128)(2,1)S(1)} %get-tuple-element.134), channel_id=1, source_target_pairs={{0,14},{1,13},{2,12},{3,11},{4,10},{5,9},{6,8},{7,7},{8,6},{9,5},{... | collective-permute-start | bytes 13832 | tf_op jit(solution)/shard_map/ppermute | solution.py:31
  11.1 3.3 %collective-permute-start = (bf16[9,3,768]{2,1,0:T(4,128)(2,1)S(1)}, bf16[9,3,768]{2,1,0:T(4,128)(2,1)S(1)}, u32[]{:S(2)}, u32[]{:S(2)}) collective-permute-start(bf16[9,3,768]{2,1,0:T(4,128)(2,1)S(1)} %get-tuple-element.118), channel_id=1, source_target_pairs={{0,1},{1,2},{2,3},{3,4},{4,5},{5,6},{6,7},{7,8},{8,9},{9,10},{10,1... | collective-permute-start | bytes 124424 | tf_op jit(solution)/shard_map/ppermute | solution.py:24
  16.6 2.3 %rev.3 = f32[7,7,768]{2,1,0:T(8,128)S(1)} reverse(bf16[7,7,768]{2,1,0:T(8,128)(2,1)} %param.9), dimensions={1} | reverse | bytes 225792 | tf_op jit(solution)/shard_map/rev | solution.py:162
  20.0 1.7 %collective-permute-done.1 = bf16[9,3,768]{2,1,0:T(4,128)(2,1)S(1)} collective-permute-done((bf16[9,3,768]{2,1,0:T(4,128)(2,1)S(1)}, bf16[9,3,768]{2,1,0:T(4,128)(2,1)S(1)}, u32[]{:S(2)}, u32[]{:S(2)}) %collective-permute-start.1) | collective-permute-done | bytes 41504 | tf_op jit(solution)/shard_map/ppermute | solution.py:24
  22.0 2.9 %fusion.128 = (f32[2,8,8]{2,1,0:T(8,128)S(1)}, f32[2,8,8,768]{3,2,1,0:T(8,128)S(1)}) fusion(f32[2,768]{1,0:T(2,128)S(1)} %get-tuple-element.138, f32[2,768]{1,0:T(2,128)S(1)} %get-tuple-element.142, f32[2,768]{1,0:T(2,128)S(1)} %get-tuple-element.143, f32[2,768]{1,0:T(2,128)S(1)} %get-tuple-element.144, f32[2,768]{1,0:T(2,128)S(1)} %get-tuple-element.145, ...), kind=kLoop, calls=%fused_computation.345 | loop fusion | flops 9633664 | bytes 4233728 | tf_op jit(solution)/shard_map/reduce_sum | solution.py:173
  26.2 3.7 %collective-permute-start.8 = (bf16[4,2,48,128]{3,2,1,0:T(8,128)(2,1)}, bf16[4,2,48,128]{3,2,1,0:T(8,128)(2,1)}, u32[]{:S(2)}, u32[]{:S(2)}) collective-permute-start(bf16[4,2,48,128]{3,2,1,0:T(8,128)(2,1)} %get-tuple-element.116), channel_id=1, source_target_pairs={{0,1},{1,0},{2,3},{3,2},{4,5},{5,4},{6,7},{7,6},{8,9},{9,8},{10,11... | collective-permute-start | bytes 294920 | tf_op jit(solution)/shard_map/ppermute | solution.py:13
  29.9 4.8 %fusion.127 = (f32[128,3072]{1,0:T(8,128)S(1)}, bf16[128,3072]{1,0:T(8,128)(2,1)}, f32[128,3072]{1,0:T(8,128)S(1)}) fusion(bf16[128,768]{1,0:T(8,128)(2,1)S(1)} %bitcast.204, bf16[768,3072]{1,0:T(8,128)(2,1)} %weight_ref.1), kind=kOutput, calls=%fused_computation.344 | convolution fusion | flops 608698368 | bytes 8847360 | tf_op jit(solution)/shard_map/dot_general | solution.py:179
  35.4 1.6 %reshape.125 = bf16[4,2,2,192,64]{3,2,1,0,4:T(2,128)(2,1)S(1)} reshape(bf16[3072,64]{0,1:T(8,128)(2,1)} %fusion.11) | data formatting | bytes 786432 | tf_op jit(solution)/shard_map/reshape | solution.py:184
  37.0 2.0 %constant_dynamic-slice_fusion = (bf16[4,1,1,192,64]{3,2,1,0,4:T(2,128)(2,1)}, bf16[4,1,1,192,64]{3,2,1,0,4:T(2,128)(2,1)}, bf16[4,1,1,192,64]{3,2,1,0,4:T(2,128)(2,1)}, bf16[4,1,1,192,64]{3,2,1,0,4:T(2,128)(2,1)}) fusion(bf16[4,2,2,192,64]{3,2,1,0,4:T(2,128)(2,1)S(1)} %reshape.125, s32[]{:T(128)S(6)} %select_n.94, s32[]{:T(128)S(6)} %select_n.92, ...), kind=kLoop, calls=%fused_computation.320 | loop fusion | bytes 786448 | tf_op jit(solution)/shard_map/jit(dynamic_index_in_dim)/dynamic_slice | solution.py:41
  39.0 1.8 %copy.21 = bf16[4,1,1,192,64]{4,3,0,2,1:T(8,128)(2,1)} copy(bf16[4,1,1,192,64]{3,2,1,0,4:T(2,128)(2,1)} %get-tuple-element.57) | data formatting | bytes 196608 | tf_op jit(solution)/shard_map/jit(dynamic_index_in_dim)/dynamic_slice | solution.py:41
  40.8 1.8 %copy.20 = bf16[4,1,1,192,64]{4,3,0,2,1:T(8,128)(2,1)} copy(bf16[4,1,1,192,64]{3,2,1,0,4:T(2,128)(2,1)} %get-tuple-element.58) | data formatting | bytes 196608 | tf_op jit(solution)/shard_map/jit(dynamic_index_in_dim)/dynamic_slice | solution.py:41
  42.6 1.8 %copy.19 = bf16[4,1,1,192,64]{4,3,0,2,1:T(8,128)(2,1)} copy(bf16[4,1,1,192,64]{3,2,1,0,4:T(2,128)(2,1)} %get-tuple-element.59) | data formatting | bytes 196608 | tf_op jit(solution)/shard_map/jit(dynamic_index_in_dim)/dynamic_slice | solution.py:41
  44.4 2.1 %collective-permute-start.6 = (bf16[4,192,64]{2,1,0:T(8,128)(2,1)}, bf16[4,192,64]{2,1,0:T(8,128)(2,1)}, u32[]{:S(2)}, u32[]{:S(2)}) collective-permute-start(bf16[4,192,64]{2,1,0:T(8,128)(2,1)} %bitcast.8), channel_id=1, source_target_pairs={{0,2},{1,3},{2,0},{3,1},{4,6},{5,7},{6,4},{7,5},{8,10},{9,11},{10,... | collective-permute-start | bytes 294920 | tf_op jit(solution)/shard_map/ppermute | solution.py:13
  46.5 3.4 %fusion.132 = f32[128,768]{1,0:T(8,128)S(1)} fusion(bf16[128,3072]{1,0:T(8,128)(2,1)} %get-tuple-element.43, bf16[3072,768]{1,0:T(8,128)(2,1)} %param.12), kind=kOutput, calls=%fused_computation.348 | convolution fusion | flops 603979776 | bytes 5898240 | tf_op jit(solution)/shard_map/dot_general | solution.py:195
  52.5 3.2 %collective-permute-done.7 = bf16[4,192,64]{2,1,0:T(8,128)(2,1)} collective-permute-done((bf16[4,192,64]{2,1,0:T(8,128)(2,1)}, bf16[4,192,64]{2,1,0:T(8,128)(2,1)}, u32[]{:S(2)}, u32[]{:S(2)}) %collective-permute-start.7) | collective-permute-done | bytes 98336 | tf_op jit(solution)/shard_map/ppermute | solution.py:13
  56.5 1.6 %collective-permute-start.11 = (bf16[64,768]{1,0:T(8,128)(2,1)S(1)}, bf16[64,768]{1,0:T(8,128)(2,1)S(1)}, u32[]{:S(2)}, u32[]{:S(2)}) collective-permute-start(bf16[64,768]{1,0:T(8,128)(2,1)S(1)} %fusion.119), channel_id=1, source_target_pairs={{0,3},{1,2},{2,1},{3,0},{4,7},{5,6},{6,5},{7,4},{8,11},{9,10},{10,... | collective-permute-start | bytes 294920 | tf_op jit(solution)/shard_map/ppermute | solution.py:13
  58.5 3.9 %fusion.12 = (bf16[1,64,3072]{2,1,0:T(8,128)(2,1)S(1)}, bf16[1,64,3072]{2,1,0:T(8,128)(2,1)S(1)}) fusion(f32[128,3072]{1,0:T(8,128)S(1)} %get-tuple-element.50, bf16[64,768]{1,0:T(8,128)(2,1)S(1)} %fusion.119, bf16[3072,768]{1,0:T(8,128)(2,1)} %param.12), kind=kOutput, calls=%fused_computation.66 | convolution fusion | flops 302972928 | bytes 7176192 | tf_op jit(solution)/shard_map/dot_general | solution.py:208
  65.3 3.3 %fusion.131 = (bf16[4,192,768]{2,1,0:T(8,128)(2,1)S(1)}, f32[4,192,768]{2,1,0:T(8,128)}) fusion(bf16[64,768]{1,0:T(8,128)(2,1)S(1)} %collective-permute-done.11, bf16[64,768]{1,0:T(8,128)(2,1)S(1)} %collective-permute-done.10, bf16[64,768]{1,0:T(8,128)(2,1)S(1)} %collective-permute-done.9, bf16[64,768]{1,0:T(8,128)(2,1)S(1)} %fusion.119, ...), kind=kOutput, calls=%fused_computation.347 | convolution fusion | flops 305725440 | bytes 4325376 | tf_op jit(solution)/shard_map/dot_general | solution.py:218
  69.3 2.0 %collective-permute-start.15 = (bf16[192,768]{1,0:T(8,128)(2,1)S(1)}, bf16[192,768]{1,0:T(8,128)(2,1)S(1)}, u32[]{:S(2)}, u32[]{:S(2)}) collective-permute-start(bf16[192,768]{1,0:T(8,128)(2,1)S(1)} %get-tuple-element.55), channel_id=1, source_target_pairs={{0,8},{1,9},{2,10},{3,11},{4,12},{5,13},{6,14},{7,15},{8,0},{9,1},... | collective-permute-start | bytes 884744 | tf_op jit(solution)/shard_map/ppermute | solution.py:13
  71.4 1.5 %convolution_convert_fusion = bf16[192,3072]{1,0:T(8,128)(2,1)} fusion(bf16[192,256]{1,0:T(8,128)(2,1)S(1)} %bitcast.207, bf16[256,3072]{1,0:T(8,128)(2,1)S(1)} %constant_dynamic-update-slice_fusion), kind=kOutput, calls=%fused_computation.43 | convolution fusion | flops 302579712 | bytes 2850816 | tf_op jit(solution)/shard_map/dot_general | solution.py:229
  73.7 4.9 %shard_map.118 = f32[64,768]{1,0:T(8,128)S(1)} custom-call(bf16[128,3072]{1,0:T(8,128)(2,1)S(1)} %bitcast.190, bf16[768,3072]{1,0:T(8,128)(2,1)S(1)} %bitcast.187, f32[128,768]{1,0:T(8,128)S(1)} %bitcast.191, f32[128,1]{1,0:T(8,128)S(1)} %rsqrt.20.inverse_ref, f32[1,768]{1,0:T(1,128)S(1)} %broadcast_in_dim.7.gain_ref, ...), custom_call_target="tpu_custom_call" | custom-call | flops 20000000000 | bytes 30000000 | tf_op jit(solution)/shard_map/pallas_call | solution.py:111
  78.6 19.0 %collective-permute-done.15 = bf16[192,768]{1,0:T(8,128)(2,1)S(1)} collective-permute-done((bf16[192,768]{1,0:T(8,128)(2,1)S(1)}, bf16[192,768]{1,0:T(8,128)(2,1)S(1)}, u32[]{:S(2)}, u32[]{:S(2)}) %collective-permute-start.15) | collective-permute-done | bytes 294944 | tf_op jit(solution)/shard_map/ppermute | solution.py:13
  99.1 4.8 %collective-permute-done.18 = f32[32,768]{1,0:T(8,128)S(1)} collective-permute-done((f32[32,768]{1,0:T(8,128)S(1)}, f32[32,768]{1,0:T(8,128)S(1)}, u32[]{:S(2)}, u32[]{:S(2)}) %collective-permute-start.18) | collective-permute-done | bytes 98336 | tf_op jit(solution)/shard_map/ppermute | solution.py:13
  105.0 2.3 %fusion.8 = f32[192,768]{1,0:T(8,128)} fusion(bf16[192,768]{1,0:T(8,128)(2,1)} %copy-done.3, bf16[192,768]{1,0:T(8,128)(2,1)} %copy-done.4, bf16[192,768]{1,0:T(8,128)(2,1)} %copy-done.5, f32[4,192,768]{2,1,0:T(8,128)} %get-tuple-element.137, s32[]{:T(128)S(6)} %select_n.103), kind=kLoop, calls=%fused_computation.61 | loop fusion | flops 884736 | bytes 2064388 | tf_op jit(solution)/shard_map/add | solution.py:57
  107.2 3.8 %collective-permute-done.19 = f32[32,768]{1,0:T(8,128)S(1)} collective-permute-done((f32[32,768]{1,0:T(8,128)S(1)}, f32[32,768]{1,0:T(8,128)S(1)}, u32[]{:S(2)}, u32[]{:S(2)}) %collective-permute-start.19) | collective-permute-done | bytes 98336 | tf_op jit(solution)/shard_map/ppermute | solution.py:13
  111.8 1.9 %convolution_add_fusion = f32[192,3072]{1,0:T(8,128)S(1)} fusion(bf16[192,256]{1,0:T(8,128)(2,1)} %bitcast.208, bf16[256,3072]{1,0:T(8,128)(2,1)} %copy-done, bf16[192,3072]{1,0:T(8,128)(2,1)S(1)} %collective-permute-done.13), kind=kOutput, calls=%fused_computation.42 | convolution fusion | flops 303169536 | bytes 5210112 | tf_op jit(solution)/shard_map/dot_general | solution.py:229
  114.0 1.8 %collective-permute-done.23 = f32[32,768]{1,0:T(8,128)S(1)} collective-permute-done((f32[32,768]{1,0:T(8,128)S(1)}, f32[32,768]{1,0:T(8,128)S(1)}, u32[]{:S(2)}, u32[]{:S(2)}) %collective-permute-start.23) | collective-permute-done | bytes 98336 | tf_op jit(solution)/shard_map/ppermute | solution.py:13
  116.8 3.8 %collective-permute-start.22 = (bf16[48,3072]{1,0:T(8,128)(2,1)}, bf16[48,3072]{1,0:T(8,128)(2,1)S(1)}, u32[]{:S(2)}, u32[]{:S(2)}) collective-permute-start(bf16[48,3072]{1,0:T(8,128)(2,1)} %get-tuple-element.52), channel_id=1, source_target_pairs={{0,12},{1,13},{2,14},{3,15},{4,0},{5,1},{6,2},{7,3},{8,4},{9,5},{1... | collective-permute-start | bytes 884744 | tf_op jit(solution)/shard_map/ppermute | solution.py:13
  122.0 6.7 %collective-permute-done.20 = bf16[48,3072]{1,0:T(8,128)(2,1)S(1)} collective-permute-done((bf16[48,3072]{1,0:T(8,128)(2,1)}, bf16[48,3072]{1,0:T(8,128)(2,1)S(1)}, u32[]{:S(2)}, u32[]{:S(2)}) %collective-permute-start.20) | collective-permute-done | bytes 294944 | tf_op jit(solution)/shard_map/ppermute | solution.py:13
  128.7 6.5 %collective-permute-done.22 = bf16[48,3072]{1,0:T(8,128)(2,1)S(1)} collective-permute-done((bf16[48,3072]{1,0:T(8,128)(2,1)}, bf16[48,3072]{1,0:T(8,128)(2,1)S(1)}, u32[]{:S(2)}, u32[]{:S(2)}) %collective-permute-start.22) | collective-permute-done | bytes 294944 | tf_op jit(solution)/shard_map/ppermute | solution.py:13
  135.2 9.8 %collective-permute-done.21 = bf16[48,3072]{1,0:T(8,128)(2,1)S(1)} collective-permute-done((bf16[48,3072]{1,0:T(8,128)(2,1)}, bf16[48,3072]{1,0:T(8,128)(2,1)S(1)}, u32[]{:S(2)}, u32[]{:S(2)}) %collective-permute-start.21) | collective-permute-done | bytes 294944 | tf_op jit(solution)/shard_map/ppermute | solution.py:13
  (131 shorter events, 22.5 us)
Async XLA Ops:
  0.6 19.2 %collective-permute-start.3 = (bf16[8,768]{1,0:T(8,128)(2,1)}, bf16[8,768]{1,0:T(8,128)(2,1)S(1)}, u32[]{:S(2)}, u32[]{:S(2)}) collective-permute-start(bf16[8,768]{1,0:T(8,128)(2,1)} %param.8), channel_id=1, source_target_pairs={{0,15},{1,14},{2,13},{3,12},{4,11},{5,10},{6,9},{7,8},{8,7},{9,6},... | collective-permute-start | bytes 36872 | tf_op jit(solution)/shard_map/ppermute | solution.py:31
  6.9 12.9 %collective-permute-start.2 = (bf16[3,768]{1,0:T(4,128)(2,1)S(1)}, bf16[3,768]{1,0:T(4,128)(2,1)S(1)}, u32[]{:S(2)}, u32[]{:S(2)}) collective-permute-start(bf16[3,768]{1,0:T(4,128)(2,1)S(1)} %get-tuple-element.134), channel_id=1, source_target_pairs={{0,14},{1,13},{2,12},{3,11},{4,10},{5,9},{6,8},{7,7},{8,6},{9,5},{... | collective-permute-start | bytes 13832 | tf_op jit(solution)/shard_map/ppermute | solution.py:31
  9.4 10.4 %collective-permute-start.4 = (bf16[3,768]{1,0:T(4,128)(2,1)S(1)}, bf16[3,768]{1,0:T(4,128)(2,1)S(1)}, u32[]{:S(2)}, u32[]{:S(2)}) collective-permute-start(bf16[3,768]{1,0:T(4,128)(2,1)S(1)} %get-tuple-element.135), channel_id=1, source_target_pairs={{1,15},{2,14},{3,13},{4,12},{5,11},{6,10},{7,9},{8,8},{9,7},{10,6}... | collective-permute-start | bytes 13832 | tf_op jit(solution)/shard_map/ppermute | solution.py:31
  11.1 8.9 %collective-permute-start = (bf16[9,3,768]{2,1,0:T(4,128)(2,1)S(1)}, bf16[9,3,768]{2,1,0:T(4,128)(2,1)S(1)}, u32[]{:S(2)}, u32[]{:S(2)}) collective-permute-start(bf16[9,3,768]{2,1,0:T(4,128)(2,1)S(1)} %get-tuple-element.118), channel_id=1, source_target_pairs={{0,1},{1,2},{2,3},{3,4},{4,5},{5,6},{6,7},{7,8},{8,9},{9,10},{10,1... | collective-permute-start | bytes 124424 | tf_op jit(solution)/shard_map/ppermute | solution.py:24
  14.4 7.3 %collective-permute-start.1 = (bf16[9,3,768]{2,1,0:T(4,128)(2,1)S(1)}, bf16[9,3,768]{2,1,0:T(4,128)(2,1)S(1)}, u32[]{:S(2)}, u32[]{:S(2)}) collective-permute-start(bf16[9,3,768]{2,1,0:T(4,128)(2,1)S(1)} %get-tuple-element.119), channel_id=1, source_target_pairs={{1,0},{2,1},{3,2},{4,3},{5,4},{6,5},{7,6},{8,7},{9,8},{10,9},{11,1... | collective-permute-start | bytes 124424 | tf_op jit(solution)/shard_map/ppermute | solution.py:24
  18.9 2.8 %copy-start.1 = (bf16[8,8,768]{2,1,0:T(8,128)(2,1)S(1)}, bf16[8,8,768]{2,1,0:T(8,128)(2,1)}, u32[]{:S(2)}) copy-start(bf16[8,8,768]{2,1,0:T(8,128)(2,1)} %param.7) | copy-start | bytes 294916
  18.9 2.8 %copy-start.6 = (bf16[8,768]{1,0:T(8,128)(2,1)S(1)}, bf16[8,768]{1,0:T(8,128)(2,1)}, u32[]{:S(2)}) copy-start(bf16[8,768]{1,0:T(8,128)(2,1)} %param.8) | copy-start | bytes 36868
  26.2 37.6 %collective-permute-start.8 = (bf16[4,2,48,128]{3,2,1,0:T(8,128)(2,1)}, bf16[4,2,48,128]{3,2,1,0:T(8,128)(2,1)}, u32[]{:S(2)}, u32[]{:S(2)}) collective-permute-start(bf16[4,2,48,128]{3,2,1,0:T(8,128)(2,1)} %get-tuple-element.116), channel_id=1, source_target_pairs={{0,1},{1,0},{2,3},{3,2},{4,5},{5,4},{6,7},{7,6},{8,9},{9,8},{10,11... | collective-permute-start | bytes 294920 | tf_op jit(solution)/shard_map/ppermute | solution.py:13
  44.4 6.7 %collective-permute-start.5 = (bf16[4,192,64]{2,1,0:T(8,128)(2,1)}, bf16[4,192,64]{2,1,0:T(8,128)(2,1)}, u32[]{:S(2)}, u32[]{:S(2)}) collective-permute-start(bf16[4,192,64]{2,1,0:T(8,128)(2,1)} %bitcast.7), channel_id=1, source_target_pairs={{0,1},{1,0},{2,3},{3,2},{4,5},{5,4},{6,7},{7,6},{8,9},{9,8},{10,11... | collective-permute-start | bytes 294920 | tf_op jit(solution)/shard_map/ppermute | solution.py:13
  44.4 8.1 %collective-permute-start.6 = (bf16[4,192,64]{2,1,0:T(8,128)(2,1)}, bf16[4,192,64]{2,1,0:T(8,128)(2,1)}, u32[]{:S(2)}, u32[]{:S(2)}) collective-permute-start(bf16[4,192,64]{2,1,0:T(8,128)(2,1)} %bitcast.8), channel_id=1, source_target_pairs={{0,2},{1,3},{2,0},{3,1},{4,6},{5,7},{6,4},{7,5},{8,10},{9,11},{10,... | collective-permute-start | bytes 294920 | tf_op jit(solution)/shard_map/ppermute | solution.py:13
  46.5 9.2 %collective-permute-start.7 = (bf16[4,192,64]{2,1,0:T(8,128)(2,1)}, bf16[4,192,64]{2,1,0:T(8,128)(2,1)}, u32[]{:S(2)}, u32[]{:S(2)}) collective-permute-start(bf16[4,192,64]{2,1,0:T(8,128)(2,1)} %bitcast.9), channel_id=1, source_target_pairs={{0,3},{1,2},{2,1},{3,0},{4,7},{5,6},{6,5},{7,4},{8,11},{9,10},{10,... | collective-permute-start | bytes 294920 | tf_op jit(solution)/shard_map/ppermute | solution.py:13
  46.5 9.2 %copy-start.7 = (f32[768]{0:T(1024)S(1)}, f32[768]{0:T(1024)}, u32[]{:S(2)}) copy-start(f32[768]{0:T(1024)} %param.13) | copy-start | bytes 9220
  56.5 6.0 %collective-permute-start.11 = (bf16[64,768]{1,0:T(8,128)(2,1)S(1)}, bf16[64,768]{1,0:T(8,128)(2,1)S(1)}, u32[]{:S(2)}, u32[]{:S(2)}) collective-permute-start(bf16[64,768]{1,0:T(8,128)(2,1)S(1)} %fusion.119), channel_id=1, source_target_pairs={{0,3},{1,2},{2,1},{3,0},{4,7},{5,6},{6,5},{7,4},{8,11},{9,10},{10,... | collective-permute-start | bytes 294920 | tf_op jit(solution)/shard_map/ppermute | solution.py:13
  58.1 5.7 %collective-permute-start.10 = (bf16[64,768]{1,0:T(8,128)(2,1)S(1)}, bf16[64,768]{1,0:T(8,128)(2,1)S(1)}, u32[]{:S(2)}, u32[]{:S(2)}) collective-permute-start(bf16[64,768]{1,0:T(8,128)(2,1)S(1)} %fusion.119), channel_id=1, source_target_pairs={{0,2},{1,3},{2,0},{3,1},{4,6},{5,7},{6,4},{7,5},{8,10},{9,11},{10,... | collective-permute-start | bytes 294920 | tf_op jit(solution)/shard_map/ppermute | solution.py:13
  58.5 5.3 %collective-permute-start.9 = (bf16[64,768]{1,0:T(8,128)(2,1)S(1)}, bf16[64,768]{1,0:T(8,128)(2,1)S(1)}, u32[]{:S(2)}, u32[]{:S(2)}) collective-permute-start(bf16[64,768]{1,0:T(8,128)(2,1)S(1)} %fusion.119), channel_id=1, source_target_pairs={{0,1},{1,0},{2,3},{3,2},{4,5},{5,4},{6,7},{7,6},{8,9},{9,8},{10,11... | collective-permute-start | bytes 294920 | tf_op jit(solution)/shard_map/ppermute | solution.py:13
  63.8 7.6 %collective-permute-start.12 = (bf16[128,3072]{1,0:T(8,128)(2,1)S(1)}, bf16[128,3072]{1,0:T(8,128)(2,1)S(1)}, u32[]{:S(2)}, u32[]{:S(2)}) collective-permute-start(bf16[128,3072]{1,0:T(8,128)(2,1)S(1)} %bitcast.188), channel_id=1, source_target_pairs={{0,1},{1,0},{2,3},{3,2},{4,5},{5,4},{6,7},{7,6},{8,9},{9,8},{10,11... | collective-permute-start | bytes 2359304 | tf_op jit(solution)/shard_map/ppermute | solution.py:13
  65.3 8.4 %slice-start = ((s8[4718592]{0:T(1024)(128)(4,1)}), s8[4194304]{0:T(1024)(128)(4,1)S(1)}, s32[]{:S(2)}) async-start(s8[4718592]{0:T(1024)(128)(4,1)} %bitcast.186), calls=%async_computation | async-start | bytes 8388608
  68.6 5.1 %slice-start.1 = ((s8[4718592]{0:T(1024)(128)(4,1)}), s8[524288]{0:T(1024)(128)(4,1)S(1)}, s32[]{:S(2)}) async-start(s8[4718592]{0:T(1024)(128)(4,1)} %bitcast.186), calls=%async_computation.1 | async-start | bytes 1048576
  68.6 10.0 %collective-permute-start.16 = (bf16[192,768]{1,0:T(8,128)(2,1)S(1)}, bf16[192,768]{1,0:T(8,128)(2,1)S(1)}, u32[]{:S(2)}, u32[]{:S(2)}) collective-permute-start(bf16[192,768]{1,0:T(8,128)(2,1)S(1)} %get-tuple-element.54), channel_id=1, source_target_pairs={{0,12},{1,13},{2,14},{3,15},{4,0},{5,1},{6,2},{7,3},{8,4},{9,5},{1... | collective-permute-start | bytes 884744 | tf_op jit(solution)/shard_map/ppermute | solution.py:13
  69.3 28.4 %collective-permute-start.15 = (bf16[192,768]{1,0:T(8,128)(2,1)S(1)}, bf16[192,768]{1,0:T(8,128)(2,1)S(1)}, u32[]{:S(2)}, u32[]{:S(2)}) collective-permute-start(bf16[192,768]{1,0:T(8,128)(2,1)S(1)} %get-tuple-element.55), channel_id=1, source_target_pairs={{0,8},{1,9},{2,10},{3,11},{4,12},{5,13},{6,14},{7,15},{8,0},{9,1},... | collective-permute-start | bytes 884744 | tf_op jit(solution)/shard_map/ppermute | solution.py:13
  71.3 26.3 %collective-permute-start.14 = (bf16[192,768]{1,0:T(8,128)(2,1)S(1)}, bf16[192,768]{1,0:T(8,128)(2,1)S(1)}, u32[]{:S(2)}, u32[]{:S(2)}) collective-permute-start(bf16[192,768]{1,0:T(8,128)(2,1)S(1)} %get-tuple-element.56), channel_id=1, source_target_pairs={{0,4},{1,5},{2,6},{3,7},{4,8},{5,9},{6,10},{7,11},{8,12},{9,13},{1... | collective-permute-start | bytes 884744 | tf_op jit(solution)/shard_map/ppermute | solution.py:13
  71.4 2.2 %copy-start = (bf16[256,3072]{1,0:T(8,128)(2,1)}, bf16[256,3072]{1,0:T(8,128)(2,1)S(1)}, u32[]{:S(2)}) copy-start(bf16[256,3072]{1,0:T(8,128)(2,1)S(1)} %constant_dynamic-update-slice_fusion) | copy-start | bytes 4718596
  73.0 38.1 %collective-permute-start.13 = (bf16[192,3072]{1,0:T(8,128)(2,1)}, bf16[192,3072]{1,0:T(8,128)(2,1)S(1)}, u32[]{:S(2)}, u32[]{:S(2)}) collective-permute-start(bf16[192,3072]{1,0:T(8,128)(2,1)} %convolution_convert_fusion), channel_id=1, source_target_pairs={{0,2},{1,3},{2,0},{3,1},{4,6},{5,7},{6,4},{7,5},{8,10},{9,11},{10,... | collective-permute-start | bytes 3538952 | tf_op jit(solution)/shard_map/ppermute | solution.py:13
  78.6 20.4 %copy-start.3 = (bf16[192,768]{1,0:T(8,128)(2,1)}, bf16[192,768]{1,0:T(8,128)(2,1)S(1)}, u32[]{:S(2)}) copy-start(bf16[192,768]{1,0:T(8,128)(2,1)S(1)} %collective-permute-done.16) | copy-start | bytes 884740
  97.6 1.4 collective-permute-start.17
  99.1 4.9 %collective-permute-start.18 = (f32[32,768]{1,0:T(8,128)S(1)}, f32[32,768]{1,0:T(8,128)S(1)}, u32[]{:S(2)}, u32[]{:S(2)}) collective-permute-start(f32[32,768]{1,0:T(8,128)S(1)} %bitcast_add_fusion.2), channel_id=1, source_target_pairs={{0,4},{1,5},{2,6},{3,7},{4,0},{5,1},{6,2},{7,3},{8,12},{9,13},{10,... | collective-permute-start | bytes 294920 | tf_op jit(solution)/shard_map/ppermute | solution.py:13
  104.0 7.1 %collective-permute-start.19 = (f32[32,768]{1,0:T(8,128)S(1)}, f32[32,768]{1,0:T(8,128)S(1)}, u32[]{:S(2)}, u32[]{:S(2)}) collective-permute-start(f32[32,768]{1,0:T(8,128)S(1)} %add.396), channel_id=1, source_target_pairs={{0,8},{1,9},{2,10},{3,11},{4,12},{5,13},{6,14},{7,15},{8,0},{9,1},... | collective-permute-start | bytes 294920 | tf_op jit(solution)/shard_map/ppermute | solution.py:13
  111.1 4.7 %collective-permute-start.23 = (f32[32,768]{1,0:T(8,128)S(1)}, f32[32,768]{1,0:T(8,128)S(1)}, u32[]{:S(2)}, u32[]{:S(2)}) collective-permute-start(f32[32,768]{1,0:T(8,128)S(1)} %add.397), channel_id=1, source_target_pairs={{0,2},{1,3},{2,0},{3,1},{4,6},{5,7},{6,4},{7,5},{8,10},{9,11},{10,... | collective-permute-start | bytes 294920 | tf_op jit(solution)/shard_map/ppermute | solution.py:13
  115.8 4.8 %collective-permute-start.24 = (f32[32,768]{1,0:T(8,128)S(1)}, f32[32,768]{1,0:T(8,128)S(1)}, u32[]{:S(2)}, u32[]{:S(2)}) collective-permute-start(f32[32,768]{1,0:T(8,128)S(1)} %add.406), channel_id=1, source_target_pairs={{0,1},{1,0},{2,3},{3,2},{4,5},{5,4},{6,7},{7,6},{8,9},{9,8},{10,11... | collective-permute-start | bytes 294920 | tf_op jit(solution)/shard_map/ppermute | solution.py:13
  116.8 11.9 %collective-permute-start.20 = (bf16[48,3072]{1,0:T(8,128)(2,1)}, bf16[48,3072]{1,0:T(8,128)(2,1)S(1)}, u32[]{:S(2)}, u32[]{:S(2)}) collective-permute-start(bf16[48,3072]{1,0:T(8,128)(2,1)} %get-tuple-element.51), channel_id=1, source_target_pairs={{0,4},{1,5},{2,6},{3,7},{4,8},{5,9},{6,10},{7,11},{8,12},{9,13},{1... | collective-permute-start | bytes 884744 | tf_op jit(solution)/shard_map/ppermute | solution.py:13
  116.8 18.3 %collective-permute-start.22 = (bf16[48,3072]{1,0:T(8,128)(2,1)}, bf16[48,3072]{1,0:T(8,128)(2,1)S(1)}, u32[]{:S(2)}, u32[]{:S(2)}) collective-permute-start(bf16[48,3072]{1,0:T(8,128)(2,1)} %get-tuple-element.52), channel_id=1, source_target_pairs={{0,12},{1,13},{2,14},{3,15},{4,0},{5,1},{6,2},{7,3},{8,4},{9,5},{1... | collective-permute-start | bytes 884744 | tf_op jit(solution)/shard_map/ppermute | solution.py:13
  120.7 24.3 %collective-permute-start.21 = (bf16[48,3072]{1,0:T(8,128)(2,1)}, bf16[48,3072]{1,0:T(8,128)(2,1)S(1)}, u32[]{:S(2)}, u32[]{:S(2)}) collective-permute-start(bf16[48,3072]{1,0:T(8,128)(2,1)} %get-tuple-element.53), channel_id=1, source_target_pairs={{0,8},{1,9},{2,10},{3,11},{4,12},{5,13},{6,14},{7,15},{8,0},{9,1},... | collective-permute-start | bytes 884744 | tf_op jit(solution)/shard_map/ppermute | solution.py:13
  (4 other events, 5.1 us)

commit v4 on v2

--- a/solution.py
+++ b/solution.py
@@ -17,6 +17,10 @@
     normal_cdf = 0.5 * (1.0 + jax.scipy.special.erf(pre * 0.7071067811865476))
     density = jnp.exp(-0.5 * pre * pre) * 0.3989422804014327
     return (pre * normal_cdf, normal_cdf + pre * density)
+
+
+def rounded_f32(value):
+    return lax.reduce_precision(value, 8, 7)
 
 
 def with_halo(block, width):
@@ -63,6 +67,7 @@
     nhat = nhat_ref[...]
     out_ref[49:50] = jnp.sum(dnormed * nhat, axis=0, keepdims=True)
     out_ref[50:51] = scale_ref[...]
+    out_ref[51:64] = jnp.zeros((13, channels), jnp.float32)
     scaled = dnormed * gain_ref[...]
     dconv = inverse_ref[...] * (
         scaled
@@ -100,7 +105,7 @@
     view_count, rows, wide, _ = widened.shape
     return pl.pallas_call(
         tail_kernel,
-        out_shape=jax.ShapeDtypeStruct((51, channels), jnp.float32),
+        out_shape=jax.ShapeDtypeStruct((64, channels), jnp.float32),
         scratch_shapes=[pltpu.VMEM((view_count, rows, wide - 6, channels), jnp.float32)],
         compiler_params=pltpu.CompilerParams(vmem_limit_bytes=32 << 20),
         cost_estimate=pl.CostEstimate(
@@ -121,13 +126,6 @@
     return lax.optimization_barrier((value, *others))[0]
 
 
-def all_sum(block):
-    count = lax.axis_size("col")
-    for bit in range(count.bit_length() - 1):
-        block = block + permuted(block, lambda i: i ^ (1 << bit))
-    return block
-
-
 def on_device(
     features, column_table, dw_kernel, norm_gain, expand_weight, reduce_weight, layer_scale
 ):
@@ -143,15 +141,16 @@
 
     mirrored_table = permuted(column_table, lambda i: count - 1 - i)[::-1]
     tables = jnp.stack([column_table, mirrored_table]).astype(jnp.float32)
-    views = (features.astype(jnp.float32)[None] + tables[:, None]).astype(jnp.bfloat16)
+    view_values = rounded_f32(features.astype(jnp.float32)[None] + tables[:, None])
+    views = view_values.astype(jnp.bfloat16)
     kernel_f = dw_kernel.astype(jnp.float32)
-    kernels = jnp.stack([kernel_f, kernel_f[:, ::-1]])
     widened = with_halo(views, 3)
     padded = jnp.pad(widened.astype(jnp.float32), ((0, 0), (3, 3), (0, 0), (0, 0)))
     conv = jnp.zeros((2, row_count, col_count, channels), jnp.float32)
     for row_off in range(7):
         for col_off in range(7):
-            weights_here = kernels[:, row_off, col_off][:, None, None, :]
+            weights_here = jnp.stack([kernel_f[row_off, col_off], kernel_f[row_off, 6 - col_off]])
+            weights_here = weights_here[:, None, None, :]
             conv = (
                 conv
                 + weights_here
@@ -165,12 +164,10 @@
     normed = (nhat * norm_gain).astype(jnp.bfloat16).reshape(-1, channels)
     pre = jnp.dot(normed, expand_weight, preferred_element_type=jnp.float32)
     activated, gelu_slope = gelu_parts(pre)
-    hidden = lax.reduce_precision(activated, 8, 7).astype(jnp.bfloat16)
+    hidden = rounded_f32(activated).astype(jnp.bfloat16)
     branch = jnp.dot(hidden, reduce_weight, preferred_element_type=jnp.float32)
-    outputs = (views.astype(jnp.float32) + layer_scale * branch.reshape(conv.shape)).astype(
-        jnp.bfloat16
-    )
-    difference = outputs[0].astype(jnp.float32) - outputs[1].astype(jnp.float32)
+    outputs = rounded_f32(view_values + layer_scale * branch.reshape(conv.shape))
+    difference = outputs[0] - outputs[1]
     disagreement = difference.astype(jnp.bfloat16)
     residual = (difference * (1.0 / math.sqrt(row_count * total_cols))).astype(jnp.bfloat16)
     residual = lax.optimization_barrier(residual)
@@ -188,33 +185,37 @@
         [pick(contrast_t, core, 2), permuted(pick(contrast_t, 1 - core, 2), other_core)], axis=-1
     )
     dbranch_pair = jnp.concatenate([dbranch, permuted(dbranch, other_core)], axis=0)
-    contrast_quad = jnp.concatenate(
-        [pick(contrast_pair, side, 1), permuted(pick(contrast_pair, 1 - side, 1), other_side)],
-        axis=-1,
-    )
-    dbranch_quad = jnp.concatenate([dbranch_pair, permuted(dbranch_pair, other_side)], axis=0)
+    contrast_near = pick(contrast_pair, side, 1)
+    contrast_far = permuted(pick(contrast_pair, 1 - side, 1), other_side)
+    dbranch_far = permuted(dbranch_pair, other_side)
+
+    dhidden = lax.dot_general(
+        dbranch, reduce_weight, (((1,), (1,)), ((), ())), preferred_element_type=jnp.float32
+    )
+    slopes = gelu_slope.reshape(2, pixels, hidden_size)
+    dpre = jnp.stack([dhidden * slopes[0], -dhidden * slopes[1]]).astype(jnp.bfloat16)
+    dpre = dpre.reshape(2 * pixels, hidden_size)
+
+    normed_t = normed.T.reshape(outer, 2, 2, channels // count, 2 * pixels)
+    normed_pair = jnp.concatenate(
+        [pick(normed_t, core, 2), permuted(pick(normed_t, 1 - core, 2), other_core)], axis=-1
+    )
+    dpre_pair = jnp.concatenate([dpre, permuted(dpre, other_core)], axis=0)
+
+    def expand_part(which):
+        rows = pick(normed_pair, which, 1).reshape(-1, 4 * pixels)
+        return jnp.dot(rows, dpre_pair, preferred_element_type=jnp.float32)
+
+    leaving = expand_part(1 - side).astype(jnp.bfloat16)
+    arrived = permuted(leaving, other_side)
+    contrast_near, dbranch_pair, _ = lax.optimization_barrier(
+        (contrast_near, dbranch_pair, leaving)
+    )
+    contrast_quad = jnp.concatenate([contrast_near, contrast_far], axis=-1)
+    dbranch_quad = jnp.concatenate([dbranch_pair, dbranch_far], axis=0)
     reduce_quad = jnp.dot(
         contrast_quad.reshape(-1, 4 * pixels), dbranch_quad, preferred_element_type=jnp.float32
     ).reshape(outer, hidden_size // count, channels)
-    dhidden = lax.dot_general(
-        dbranch, reduce_weight, (((1,), (1,)), ((), ())), preferred_element_type=jnp.float32
-    )
-    slopes = gelu_slope.reshape(2, pixels, hidden_size)
-    dpre = jnp.stack([dhidden * slopes[0], -dhidden * slopes[1]]).astype(jnp.bfloat16)
-    dpre = dpre.reshape(2 * pixels, hidden_size)
-
-    normed_t = normed.T.reshape(outer, 2, 2, channels // count, 2 * pixels)
-    normed_pair = jnp.concatenate(
-        [pick(normed_t, core, 2), permuted(pick(normed_t, 1 - core, 2), other_core)], axis=-1
-    )
-    dpre_pair = jnp.concatenate([dpre, permuted(dpre, other_core)], axis=0)
-
-    def expand_part(which):
-        rows = pick(normed_pair, which, 1).reshape(-1, 4 * pixels)
-        return jnp.dot(rows, dpre_pair, preferred_element_type=jnp.float32)
-
-    leaving = expand_part(1 - side).astype(jnp.bfloat16)
-    arrived = permuted(leaving, other_side)
     reduce_rounded = reduce_quad.astype(jnp.bfloat16)
     reduce_arrived = outer_exchange(reduce_rounded)
     small = tail(
@@ -226,12 +227,25 @@
         grad_scale_local,
         widened,
     )
-    arrived, small, *reduce_arrived = lax.optimization_barrier((arrived, small, *reduce_arrived))
+    small, reduce_arrived[0] = lax.optimization_barrier((small, reduce_arrived[0]))
+    halves = small.reshape(2, -1, channels)
+    half = pick(halves, core, 0) + permuted(pick(halves, 1 - core, 0), other_core)
+    half_rounded = half.astype(jnp.bfloat16)
+    half_arrived = [
+        permuted(half_rounded, lambda i: (i + 4 * step) % count) for step in range(1, outer)
+    ]
+    arrived, half_arrived = lax.optimization_barrier((arrived, half_arrived))
     expand_quad = expand_part(side) + arrived.astype(jnp.float32)
     expand_quad = expand_quad.reshape(outer, channels // count, hidden_size)
     expand_arrived = outer_exchange(expand_quad.astype(jnp.bfloat16))
     grad_reduce = outer_total(reduce_quad, reduce_arrived)
-    small = all_sum(small)
+    for block in half_arrived:
+        half = half + block.astype(jnp.float32)
+    half = half + permuted(half, other_side)
+    other_half = permuted(half, other_core)
+    small = jnp.concatenate(
+        [jnp.where(core == 0, half, other_half), jnp.where(core == 0, other_half, half)], axis=0
+    )
     grad_expand = outer_total(expand_quad, expand_arrived)
     return (
         disagreement,

time: 131 us -> 124 us (0.947)
  the two profiles are of different devices: /device:TPU:0 before, /device:TPU:9 now
where the time goes in v4:
time: 124 us; the launch traced here: 123 us
  waiting for transfers between devices  50.6 us (41%)
  starting transfers between devices  30.6 us (25%)
  other arithmetic  13.3 us (11%)
  local copies, waits for them, and re-layouts  11.4 us (9%)
  matrix products  11.2 us (9%)
  Pallas kernels  4.94 us (4%)
    ppermute x20, waiting for transfers between devices, permuted(): return lax.ppermute(block, 'col', [(i, target(i)) for i in range(count)])  46.9 us
    ppermute x20, starting transfers between devices, permuted(): return lax.ppermute(block, 'col', [(i, target(i)) for i in range(count)])  26.2 us
    pallas_call x1, Pallas kernels, tail(): pl.pallas_call(tail_kernel, out_shape=jax.ShapeDtypeStruct((64, channels)...  4.94 us
    unnamed x18, local copies, waits for them, and re-layouts  4.49 us
    dot_general x2, matrix products, expand_part(): return jnp.dot(rows, dpre_pair, preferred_element_type=jnp.float32)  4.31 us
    add x2, other arithmetic, outer_total(): total = total + block.astype(jnp.float32)  4.13 us
    ppermute x1, waiting for transfers between devices, with_halo(): high = lax.ppermute(block[:, :, :width], 'col', backward)  3.68 us
    dot_general x1, matrix products, on_device(): jnp.dot(contrast_quad.reshape(-1, 4 * pixels), dbranch_quad, preferred_el...  3.01 us
  transfers between devices with their start and end apart: 22, of which 8 were waited for; matrix products, arithmetic and copies ran while one was open for 18% of the time, Pallas kernels for 4%

profile of v4, /device:TPU:9, one launch (start us, length us, event | category | flops | bytes accessed | tf_op | source)
XLA Modules:
  0.0 123.2 jit_solution(1436915116381327249)
XLA Ops:
  0.6 2.8 %collective-permute-start = (bf16[8,768]{1,0:T(8,128)(2,1)}, bf16[8,768]{1,0:T(8,128)(2,1)S(1)}, u32[]{:S(2)}, u32[]{:S(2)}) collective-permute-start(bf16[8,768]{1,0:T(8,128)(2,1)} %param.8), channel_id=1, source_target_pairs={{0,15},{1,14},{2,13},{3,12},{4,11},{5,10},{6,9},{7,8},{8,7},{9,6},... | collective-permute-start | bytes 36872 | tf_op jit(solution)/shard_map/ppermute | solution.py:13
  7.5 2.1 %collective-permute-start.1 = (bf16[2,8,3,768]{3,2,1,0:T(4,128)(2,1)S(1)}, bf16[2,8,3,768]{3,2,1,0:T(4,128)(2,1)S(1)}, u32[]{:S(2)}, u32[]{:S(2)}) collective-permute-start(bf16[2,8,3,768]{3,2,1,0:T(4,128)(2,1)S(1)} %get-tuple-element.53), channel_id=1, source_target_pairs={{0,1},{1,2},{2,3},{3,4},{4,5},{5,6},{6,7},{7,8},{8,9},{9,10},{10,1... | collective-permute-start | bytes 221192 | tf_op jit(solution)/shard_map/ppermute | solution.py:30
  9.7 2.2 %collective-permute-start.2 = (bf16[2,8,3,768]{3,2,1,0:T(4,128)(2,1)S(1)}, bf16[2,8,3,768]{3,2,1,0:T(4,128)(2,1)S(1)}, u32[]{:S(2)}, u32[]{:S(2)}) collective-permute-start(bf16[2,8,3,768]{3,2,1,0:T(4,128)(2,1)S(1)} %get-tuple-element.54), channel_id=1, source_target_pairs={{1,0},{2,1},{3,2},{4,3},{5,4},{6,5},{7,6},{8,7},{9,8},{10,9},{11,1... | collective-permute-start | bytes 221192 | tf_op jit(solution)/shard_map/ppermute | solution.py:31
  11.9 3.7 %collective-permute-done.2 = bf16[2,8,3,768]{3,2,1,0:T(4,128)(2,1)S(1)} collective-permute-done((bf16[2,8,3,768]{3,2,1,0:T(4,128)(2,1)S(1)}, bf16[2,8,3,768]{3,2,1,0:T(4,128)(2,1)S(1)}, u32[]{:S(2)}, u32[]{:S(2)}) %collective-permute-start.2) | collective-permute-done | bytes 73760 | tf_op jit(solution)/shard_map/ppermute | solution.py:31
  15.8 2.9 %fusion.125 = (f32[2,8,8]{2,1,0:T(8,128)S(1)}, f32[2,8,8,768]{3,2,1,0:T(8,128)S(1)}) fusion(f32[2,768]{1,0:T(2,128)S(1)} %get-tuple-element.141, f32[2,768]{1,0:T(2,128)S(1)} %get-tuple-element.153, f32[2,768]{1,0:T(2,128)S(1)} %get-tuple-element.145, f32[2,768]{1,0:T(2,128)S(1)} %get-tuple-element.155, f32[2,768]{1,0:T(2,128)S(1)} %get-tuple-element.144, ...), kind=kLoop, calls=%fused_computation.329 | loop fusion | flops 9633664 | bytes 4233728 | tf_op jit(solution)/shard_map/reduce_sum | solution.py:159
  19.1 1.6 %fusion.124 = (f32[128,3072]{1,0:T(8,128)S(1)}, bf16[128,3072]{1,0:T(8,128)(2,1)S(1)}, f32[128,3072]{1,0:T(8,128)S(1)}) fusion(bf16[128,768]{1,0:T(8,128)(2,1)S(1)} %bitcast.203, bf16[768,3072]{1,0:T(8,128)(2,1)S(1)} %copy-done), kind=kOutput, calls=%fused_computation.328 | convolution fusion | flops 608698368 | bytes 8847360 | tf_op jit(solution)/shard_map/dot_general | solution.py:165
  23.5 1.5 %fusion.11 = (bf16[1,64,3072]{2,1,0:T(8,128)(2,1)S(1)}, bf16[1,64,3072]{2,1,0:T(8,128)(2,1)S(1)}) fusion(f32[128,3072]{1,0:T(8,128)S(1)} %get-tuple-element.34, bf16[64,768]{1,0:T(8,128)(2,1)S(1)} %fusion.114, bf16[3072,768]{1,0:T(8,128)(2,1)S(1)} %bitcast.199), kind=kOutput, calls=%fused_computation.69 | convolution fusion | flops 302972928 | bytes 7176192 | tf_op jit(solution)/shard_map/dot_general | solution.py:192
  26.8 1.1 constant_dynamic-slice_fusion
  29.0 1.6 %pad_maximum_fusion.4 = bf16[128,768]{1,0:T(8,128)(2,1)} fusion(bf16[64,768]{1,0:T(8,128)(2,1)} %collective-permute-done.7, bf16[64,768]{1,0:T(8,128)(2,1)S(1)} %fusion.114), kind=kLoop, calls=%fused_computation.205 | loop fusion | flops 393216 | bytes 393216 | tf_op jit(solution)/shard_map/concatenate | solution.py:187
  30.6 2.1 %collective-permute-start.9 = (bf16[128,768]{1,0:T(8,128)(2,1)}, bf16[128,768]{1,0:T(8,128)(2,1)}, u32[]{:S(2)}, u32[]{:S(2)}) collective-permute-start(bf16[128,768]{1,0:T(8,128)(2,1)} %pad_maximum_fusion.4), channel_id=1, source_target_pairs={{0,2},{1,3},{2,0},{3,1},{4,6},{5,7},{6,4},{7,5},{8,10},{9,11},{10,... | collective-permute-start | bytes 589832 | tf_op jit(solution)/shard_map/ppermute | solution.py:13
  33.9 2.7 %convolution_convert_fusion = bf16[192,3072]{1,0:T(8,128)(2,1)} fusion(bf16[192,256]{1,0:T(8,128)(2,1)S(1)} %bitcast.210, bf16[128,3072]{1,0:T(8,128)(2,1)} %collective-permute-done.4, bf16[128,3072]{1,0:T(8,128)(2,1)S(1)} %bitcast.191), kind=kOutput, calls=%fused_computation.43 | convolution fusion | flops 305725440 | bytes 2850816 | tf_op jit(solution)/shard_map/dot_general | solution.py:207
  36.5 1.4 %collective-permute-start.5 = (bf16[192,3072]{1,0:T(8,128)(2,1)}, bf16[192,3072]{1,0:T(8,128)(2,1)S(1)}, u32[]{:S(2)}, u32[]{:S(2)}) collective-permute-start(bf16[192,3072]{1,0:T(8,128)(2,1)} %convolution_convert_fusion), channel_id=1, source_target_pairs={{0,2},{1,3},{2,0},{3,1},{4,6},{5,7},{6,4},{7,5},{8,10},{9,11},{10,... | collective-permute-start | bytes 3538952 | tf_op jit(solution)/shard_map/ppermute | solution.py:13
  38.2 4.2 %collective-permute-done.8 = bf16[4,192,128]{2,1,0:T(8,128)(2,1)} collective-permute-done((bf16[4,192,128]{2,1,0:T(8,128)(2,1)}, bf16[4,192,128]{2,1,0:T(8,128)(2,1)}, u32[]{:S(2)}, u32[]{:S(2)}) %collective-permute-start.8) | collective-permute-done | bytes 196640 | tf_op jit(solution)/shard_map/ppermute | solution.py:13
  42.4 3.0 %fusion.128 = (bf16[4,192,768]{2,1,0:T(8,128)(2,1)S(1)}, f32[4,192,768]{2,1,0:T(8,128)}) fusion(bf16[128,768]{1,0:T(8,128)(2,1)} %collective-permute-done.9, bf16[128,768]{1,0:T(8,128)(2,1)} %pad_maximum_fusion.4, bf16[4,192,128]{2,1,0:T(8,128)(2,1)} %collective-permute-done.8, bf16[4,192,128]{2,1,0:T(8,128)(2,1)S(1)} %bitcast.206), kind=kOutput, calls=%fused_computation.331 | convolution fusion | flops 304152576 | bytes 4325376 | tf_op jit(solution)/shard_map/dot_general | solution.py:216
  46.3 3.2 %collective-permute-start.10 = (bf16[192,768]{1,0:T(8,128)(2,1)S(1)}, bf16[192,768]{1,0:T(8,128)(2,1)}, u32[]{:S(2)}, u32[]{:S(2)}) collective-permute-start(bf16[192,768]{1,0:T(8,128)(2,1)S(1)} %get-tuple-element.37), channel_id=1, source_target_pairs={{0,4},{1,5},{2,6},{3,7},{4,8},{5,9},{6,10},{7,11},{8,12},{9,13},{1... | collective-permute-start | bytes 884744 | tf_op jit(solution)/shard_map/ppermute | solution.py:13
  49.4 2.3 %copy-done.1 = bf16[768,3072]{1,0:T(8,128)(2,1)S(1)} copy-done((bf16[768,3072]{1,0:T(8,128)(2,1)S(1)}, bf16[768,3072]{1,0:T(8,128)(2,1)}, u32[]{:S(2)}) %copy-start.1) | copy-done | bytes 4718616
  51.8 4.9 %shard_map.118 = f32[64,768]{1,0:T(8,128)S(1)} custom-call(bf16[128,3072]{1,0:T(8,128)(2,1)S(1)} %bitcast.192, bf16[768,3072]{1,0:T(8,128)(2,1)S(1)} %copy-done.1, f32[128,768]{1,0:T(8,128)S(1)} %bitcast.197, f32[128,1]{1,0:T(8,128)S(1)} %rsqrt.20.inverse_ref, f32[1,768]{1,0:T(1,128)S(1)} %broadcast_in_dim.4.gain_ref, ...), custom_call_target="tpu_custom_call" | custom-call | flops 20000000000 | bytes 30000000 | tf_op jit(solution)/shard_map/pallas_call | solution.py:106
  56.8 1.1 collective-permute-start.11
  57.9 1.3 %collective-permute-start.18 = (bf16[192,768]{1,0:T(8,128)(2,1)}, bf16[192,768]{1,0:T(8,128)(2,1)S(1)}, u32[]{:S(2)}, u32[]{:S(2)}) collective-permute-start(bf16[192,768]{1,0:T(8,128)(2,1)} %get-tuple-element.35), channel_id=1, source_target_pairs={{0,8},{1,9},{2,10},{3,11},{4,12},{5,13},{6,14},{7,15},{8,0},{9,1},... | collective-permute-start | bytes 884744 | tf_op jit(solution)/shard_map/ppermute | solution.py:13
  60.7 2.9 %collective-permute-start.13 = (bf16[32,768]{1,0:T(8,128)(2,1)S(1)}, bf16[32,768]{1,0:T(8,128)(2,1)S(1)}, u32[]{:S(2)}, u32[]{:S(2)}) collective-permute-start(bf16[32,768]{1,0:T(8,128)(2,1)S(1)} %fusion.120), channel_id=1, source_target_pairs={{0,8},{1,9},{2,10},{3,11},{4,12},{5,13},{6,14},{7,15},{8,0},{9,1},... | collective-permute-start | bytes 147464 | tf_op jit(solution)/shard_map/ppermute | solution.py:13
  63.6 15.9 %collective-permute-done.18 = bf16[192,768]{1,0:T(8,128)(2,1)S(1)} collective-permute-done((bf16[192,768]{1,0:T(8,128)(2,1)}, bf16[192,768]{1,0:T(8,128)(2,1)S(1)}, u32[]{:S(2)}, u32[]{:S(2)}) %collective-permute-start.18) | collective-permute-done | bytes 294944 | tf_op jit(solution)/shard_map/ppermute | solution.py:13
  79.5 2.8 %collective-permute-done.19 = bf16[192,768]{1,0:T(8,128)(2,1)S(1)} collective-permute-done((bf16[192,768]{1,0:T(8,128)(2,1)}, bf16[192,768]{1,0:T(8,128)(2,1)S(1)}, u32[]{:S(2)}, u32[]{:S(2)}) %collective-permute-start.19) | collective-permute-done | bytes 294944 | tf_op jit(solution)/shard_map/ppermute | solution.py:13
  82.3 2.1 %fusion.8 = f32[192,768]{1,0:T(8,128)} fusion(bf16[192,768]{1,0:T(8,128)(2,1)S(1)} %collective-permute-done.19, bf16[192,768]{1,0:T(8,128)(2,1)S(1)} %collective-permute-done.18, bf16[192,768]{1,0:T(8,128)(2,1)} %collective-permute-done.10, f32[4,192,768]{2,1,0:T(8,128)} %get-tuple-element.147, s32[]{:T(128)S(6)} %select_n.73), kind=kLoop, calls=%fused_computation.65 | loop fusion | flops 884736 | bytes 2064388 | tf_op jit(solution)/shard_map/add | solution.py:52
  85.5 1.7 %convolution_add_fusion = f32[192,3072]{1,0:T(8,128)S(1)} fusion(bf16[192,256]{1,0:T(8,128)(2,1)S(1)} %bitcast.208, bf16[192,3072]{1,0:T(8,128)(2,1)S(1)} %collective-permute-done.5, bf16[128,3072]{1,0:T(8,128)(2,1)} %collective-permute-done.4, bf16[128,3072]{1,0:T(8,128)(2,1)S(1)} %bitcast.193), kind=kOutput, calls=%fused_computation.42 | convolution fusion | flops 306315264 | bytes 5210112 | tf_op jit(solution)/shard_map/dot_general | solution.py:207
  87.3 1.3 %copy-done.2 = f32[192,3072]{1,0:T(8,128)} copy-done((f32[192,3072]{1,0:T(8,128)}, f32[192,3072]{1,0:T(8,128)S(1)}, u32[]{:S(2)}) %copy-start.2) | copy-done | bytes 2359320
  88.6 1.7 %collective-permute-start.21 = (f32[32,768]{1,0:T(8,128)S(1)}, f32[32,768]{1,0:T(8,128)S(1)}, u32[]{:S(2)}, u32[]{:S(2)}) collective-permute-start(f32[32,768]{1,0:T(8,128)S(1)} %add.364), channel_id=1, source_target_pairs={{0,1},{1,0},{2,3},{3,2},{4,5},{5,4},{6,7},{7,6},{8,9},{9,8},{10,11... | collective-permute-start | bytes 294920 | tf_op jit(solution)/shard_map/ppermute | solution.py:13
  91.4 3.3 %collective-permute-start.16 = (bf16[48,3072]{1,0:T(8,128)(2,1)S(1)}, bf16[48,3072]{1,0:T(8,128)(2,1)S(1)}, u32[]{:S(2)}, u32[]{:S(2)}) collective-permute-start(bf16[48,3072]{1,0:T(8,128)(2,1)S(1)} %get-tuple-element.40), channel_id=1, source_target_pairs={{0,8},{1,9},{2,10},{3,11},{4,12},{5,13},{6,14},{7,15},{8,0},{9,1},... | collective-permute-start | bytes 884744 | tf_op jit(solution)/shard_map/ppermute | solution.py:13
  94.7 1.4 %collective-permute-start.17 = (bf16[48,3072]{1,0:T(8,128)(2,1)S(1)}, bf16[48,3072]{1,0:T(8,128)(2,1)S(1)}, u32[]{:S(2)}, u32[]{:S(2)}) collective-permute-start(bf16[48,3072]{1,0:T(8,128)(2,1)S(1)} %get-tuple-element.39), channel_id=1, source_target_pairs={{0,12},{1,13},{2,14},{3,15},{4,0},{5,1},{6,2},{7,3},{8,4},{9,5},{1... | collective-permute-start | bytes 884744 | tf_op jit(solution)/shard_map/ppermute | solution.py:13
  97.5 2.3 %collective-permute-done.15 = bf16[48,3072]{1,0:T(8,128)(2,1)S(1)} collective-permute-done((bf16[48,3072]{1,0:T(8,128)(2,1)S(1)}, bf16[48,3072]{1,0:T(8,128)(2,1)S(1)}, u32[]{:S(2)}, u32[]{:S(2)}) %collective-permute-start.15) | collective-permute-done | bytes 294944 | tf_op jit(solution)/shard_map/ppermute | solution.py:13
  99.7 17.0 %collective-permute-done.16 = bf16[48,3072]{1,0:T(8,128)(2,1)S(1)} collective-permute-done((bf16[48,3072]{1,0:T(8,128)(2,1)S(1)}, bf16[48,3072]{1,0:T(8,128)(2,1)S(1)}, u32[]{:S(2)}, u32[]{:S(2)}) %collective-permute-start.16) | collective-permute-done | bytes 294944 | tf_op jit(solution)/shard_map/ppermute | solution.py:13
  116.8 4.4 %collective-permute-done.17 = bf16[48,3072]{1,0:T(8,128)(2,1)S(1)} collective-permute-done((bf16[48,3072]{1,0:T(8,128)(2,1)S(1)}, bf16[48,3072]{1,0:T(8,128)(2,1)S(1)}, u32[]{:S(2)}, u32[]{:S(2)}) %collective-permute-start.17) | collective-permute-done | bytes 294944 | tf_op jit(solution)/shard_map/ppermute | solution.py:13
  121.2 2.0 %fusion.10 = f32[48,3072]{1,0:T(8,128)} fusion(bf16[48,3072]{1,0:T(8,128)(2,1)S(1)} %collective-permute-done.17, bf16[48,3072]{1,0:T(8,128)(2,1)S(1)} %collective-permute-done.16, bf16[48,3072]{1,0:T(8,128)(2,1)S(1)} %collective-permute-done.15, f32[4,48,3072]{2,1,0:T(8,128)} %bitcast.201, s32[]{:T(128)S(6)} %select_n.73), kind=kLoop, calls=%fused_computation.68 | loop fusion | flops 884736 | bytes 2064388 | tf_op jit(solution)/shard_map/add | solution.py:52
  (98 shorter events, 17.3 us)
Async XLA Ops:
  0.6 6.0 %collective-permute-start = (bf16[8,768]{1,0:T(8,128)(2,1)}, bf16[8,768]{1,0:T(8,128)(2,1)S(1)}, u32[]{:S(2)}, u32[]{:S(2)}) collective-permute-start(bf16[8,768]{1,0:T(8,128)(2,1)} %param.8), channel_id=1, source_target_pairs={{0,15},{1,14},{2,13},{3,12},{4,11},{5,10},{6,9},{7,8},{8,7},{9,6},... | collective-permute-start | bytes 36872 | tf_op jit(solution)/shard_map/ppermute | solution.py:13
  7.5 4.4 %collective-permute-start.1 = (bf16[2,8,3,768]{3,2,1,0:T(4,128)(2,1)S(1)}, bf16[2,8,3,768]{3,2,1,0:T(4,128)(2,1)S(1)}, u32[]{:S(2)}, u32[]{:S(2)}) collective-permute-start(bf16[2,8,3,768]{3,2,1,0:T(4,128)(2,1)S(1)} %get-tuple-element.53), channel_id=1, source_target_pairs={{0,1},{1,2},{2,3},{3,4},{4,5},{5,6},{6,7},{7,8},{8,9},{9,10},{10,1... | collective-permute-start | bytes 221192 | tf_op jit(solution)/shard_map/ppermute | solution.py:30
  9.7 5.9 %collective-permute-start.2 = (bf16[2,8,3,768]{3,2,1,0:T(4,128)(2,1)S(1)}, bf16[2,8,3,768]{3,2,1,0:T(4,128)(2,1)S(1)}, u32[]{:S(2)}, u32[]{:S(2)}) collective-permute-start(bf16[2,8,3,768]{3,2,1,0:T(4,128)(2,1)S(1)} %get-tuple-element.54), channel_id=1, source_target_pairs={{1,0},{2,1},{3,2},{4,3},{5,4},{6,5},{7,6},{8,7},{9,8},{10,9},{11,1... | collective-permute-start | bytes 221192 | tf_op jit(solution)/shard_map/ppermute | solution.py:31
  15.8 3.2 %copy-start.5 = (f32[768]{0:T(1024)S(1)}, f32[768]{0:T(1024)}, u32[]{:S(2)}) copy-start(f32[768]{0:T(1024)} %param.10) | copy-start | bytes 9220
  15.8 3.3 %copy-start = (bf16[768,3072]{1,0:T(8,128)(2,1)S(1)}, bf16[768,3072]{1,0:T(8,128)(2,1)}, u32[]{:S(2)}) copy-start(bf16[768,3072]{1,0:T(8,128)(2,1)} %weight_ref.1) | copy-start | bytes 14155780
  18.9 2.2 %slice-start = ((s8[4718592]{0:T(1024)(128)(4,1)}), s8[4194304]{0:T(1024)(128)(4,1)S(1)}, s32[]{:S(2)}) async-start(s8[4718592]{0:T(1024)(128)(4,1)} %bitcast.198), calls=%async_computation | async-start | bytes 8388608
  19.1 2.2 %slice-start.1 = ((s8[4718592]{0:T(1024)(128)(4,1)}), s8[524288]{0:T(1024)(128)(4,1)S(1)}, s32[]{:S(2)}) async-start(s8[4718592]{0:T(1024)(128)(4,1)} %bitcast.198), calls=%async_computation.1 | async-start | bytes 1048576
  21.3 0.8 copy-start.4
  22.9 6.1 %collective-permute-start.7 = (bf16[64,768]{1,0:T(8,128)(2,1)S(1)}, bf16[64,768]{1,0:T(8,128)(2,1)}, u32[]{:S(2)}, u32[]{:S(2)}) collective-permute-start(bf16[64,768]{1,0:T(8,128)(2,1)S(1)} %fusion.114), channel_id=1, source_target_pairs={{0,1},{1,0},{2,3},{3,2},{4,5},{5,4},{6,7},{7,6},{8,9},{9,8},{10,11... | collective-permute-start | bytes 294920 | tf_op jit(solution)/shard_map/ppermute | solution.py:13
  25.1 8.8 %collective-permute-start.4 = (bf16[128,3072]{1,0:T(8,128)(2,1)S(1)}, bf16[128,3072]{1,0:T(8,128)(2,1)}, u32[]{:S(2)}, u32[]{:S(2)}) collective-permute-start(bf16[128,3072]{1,0:T(8,128)(2,1)S(1)} %bitcast.190), channel_id=1, source_target_pairs={{0,1},{1,0},{2,3},{3,2},{4,5},{5,4},{6,7},{7,6},{8,9},{9,8},{10,11... | collective-permute-start | bytes 2359304 | tf_op jit(solution)/shard_map/ppermute | solution.py:13
  26.8 2.0 %copy-start.3 = (bf16[128,768]{0,1:T(8,128)(2,1)S(1)}, bf16[128,768]{0,1:T(8,128)(2,1)}, u32[]{:S(2)}) copy-start(bf16[128,768]{0,1:T(8,128)(2,1)} %copy.14) | copy-start | bytes 589828
  28.1 4.6 %collective-permute-start.6 = (bf16[4,2,192,64]{2,3,1,0:T(8,128)(2,1)S(1)}, bf16[4,2,192,64]{2,3,1,0:T(8,128)(2,1)S(1)}, u32[]{:S(2)}, u32[]{:S(2)}) collective-permute-start(bf16[4,2,192,64]{2,3,1,0:T(8,128)(2,1)S(1)} %bitcast.209), channel_id=1, source_target_pairs={{0,1},{1,0},{2,3},{3,2},{4,5},{5,4},{6,7},{7,6},{8,9},{9,8},{10,11... | collective-permute-start | bytes 589832 | tf_op jit(solution)/shard_map/ppermute | solution.py:13
  28.8 3.9 %collective-permute-start.3 = (bf16[4,2,48,128]{3,2,1,0:T(8,128)(2,1)S(1)}, bf16[4,2,48,128]{3,2,1,0:T(8,128)(2,1)S(1)}, u32[]{:S(2)}, u32[]{:S(2)}) collective-permute-start(bf16[4,2,48,128]{3,2,1,0:T(8,128)(2,1)S(1)} %get-tuple-element.51), channel_id=1, source_target_pairs={{0,1},{1,0},{2,3},{3,2},{4,5},{5,4},{6,7},{7,6},{8,9},{9,8},{10,11... | collective-permute-start | bytes 294920 | tf_op jit(solution)/shard_map/ppermute | solution.py:13
  30.6 7.6 %collective-permute-start.9 = (bf16[128,768]{1,0:T(8,128)(2,1)}, bf16[128,768]{1,0:T(8,128)(2,1)}, u32[]{:S(2)}, u32[]{:S(2)}) collective-permute-start(bf16[128,768]{1,0:T(8,128)(2,1)} %pad_maximum_fusion.4), channel_id=1, source_target_pairs={{0,2},{1,3},{2,0},{3,1},{4,6},{5,7},{6,4},{7,5},{8,10},{9,11},{10,... | collective-permute-start | bytes 589832 | tf_op jit(solution)/shard_map/ppermute | solution.py:13
  33.6 8.7 %collective-permute-start.8 = (bf16[4,192,128]{2,1,0:T(8,128)(2,1)}, bf16[4,192,128]{2,1,0:T(8,128)(2,1)}, u32[]{:S(2)}, u32[]{:S(2)}) collective-permute-start(bf16[4,192,128]{2,1,0:T(8,128)(2,1)} %bitcast.70), channel_id=1, source_target_pairs={{0,2},{1,3},{2,0},{3,1},{4,6},{5,7},{6,4},{7,5},{8,10},{9,11},{10,... | collective-permute-start | bytes 589832 | tf_op jit(solution)/shard_map/ppermute | solution.py:13
  36.5 47.9 %collective-permute-start.5 = (bf16[192,3072]{1,0:T(8,128)(2,1)}, bf16[192,3072]{1,0:T(8,128)(2,1)S(1)}, u32[]{:S(2)}, u32[]{:S(2)}) collective-permute-start(bf16[192,3072]{1,0:T(8,128)(2,1)} %convolution_convert_fusion), channel_id=1, source_target_pairs={{0,2},{1,3},{2,0},{3,1},{4,6},{5,7},{6,4},{7,5},{8,10},{9,11},{10,... | collective-permute-start | bytes 3538952 | tf_op jit(solution)/shard_map/ppermute | solution.py:13
  46.3 10.5 %collective-permute-start.10 = (bf16[192,768]{1,0:T(8,128)(2,1)S(1)}, bf16[192,768]{1,0:T(8,128)(2,1)}, u32[]{:S(2)}, u32[]{:S(2)}) collective-permute-start(bf16[192,768]{1,0:T(8,128)(2,1)S(1)} %get-tuple-element.37), channel_id=1, source_target_pairs={{0,4},{1,5},{2,6},{3,7},{4,8},{5,9},{6,10},{7,11},{8,12},{9,13},{1... | collective-permute-start | bytes 884744 | tf_op jit(solution)/shard_map/ppermute | solution.py:13
  49.4 2.3 %copy-start.1 = (bf16[768,3072]{1,0:T(8,128)(2,1)S(1)}, bf16[768,3072]{1,0:T(8,128)(2,1)}, u32[]{:S(2)}) copy-start(bf16[768,3072]{1,0:T(8,128)(2,1)} %weight_ref.1) | copy-start | bytes 14155780
  56.8 3.5 %collective-permute-start.11 = (f32[32,768]{1,0:T(8,128)S(1)}, f32[32,768]{1,0:T(8,128)S(1)}, u32[]{:S(2)}, u32[]{:S(2)}) collective-permute-start(f32[32,768]{1,0:T(8,128)S(1)} %dynamic-slice_bitcast_fusion.6), channel_id=1, source_target_pairs={{0,1},{1,0},{2,3},{3,2},{4,5},{5,4},{6,7},{7,6},{8,9},{9,8},{10,11... | collective-permute-start | bytes 294920 | tf_op jit(solution)/shard_map/ppermute | solution.py:13
  57.9 21.6 %collective-permute-start.18 = (bf16[192,768]{1,0:T(8,128)(2,1)}, bf16[192,768]{1,0:T(8,128)(2,1)S(1)}, u32[]{:S(2)}, u32[]{:S(2)}) collective-permute-start(bf16[192,768]{1,0:T(8,128)(2,1)} %get-tuple-element.35), channel_id=1, source_target_pairs={{0,8},{1,9},{2,10},{3,11},{4,12},{5,13},{6,14},{7,15},{8,0},{9,1},... | collective-permute-start | bytes 884744 | tf_op jit(solution)/shard_map/ppermute | solution.py:13
  59.2 23.2 %collective-permute-start.19 = (bf16[192,768]{1,0:T(8,128)(2,1)}, bf16[192,768]{1,0:T(8,128)(2,1)S(1)}, u32[]{:S(2)}, u32[]{:S(2)}) collective-permute-start(bf16[192,768]{1,0:T(8,128)(2,1)} %get-tuple-element.36), channel_id=1, source_target_pairs={{0,12},{1,13},{2,14},{3,15},{4,0},{5,1},{6,2},{7,3},{8,4},{9,5},{1... | collective-permute-start | bytes 884744 | tf_op jit(solution)/shard_map/ppermute | solution.py:13
  60.3 24.2 %collective-permute-start.12 = (bf16[32,768]{1,0:T(8,128)(2,1)S(1)}, bf16[32,768]{1,0:T(8,128)(2,1)S(1)}, u32[]{:S(2)}, u32[]{:S(2)}) collective-permute-start(bf16[32,768]{1,0:T(8,128)(2,1)S(1)} %fusion.120), channel_id=1, source_target_pairs={{0,4},{1,5},{2,6},{3,7},{4,8},{5,9},{6,10},{7,11},{8,12},{9,13},{1... | collective-permute-start | bytes 147464 | tf_op jit(solution)/shard_map/ppermute | solution.py:13
  60.7 23.7 %collective-permute-start.13 = (bf16[32,768]{1,0:T(8,128)(2,1)S(1)}, bf16[32,768]{1,0:T(8,128)(2,1)S(1)}, u32[]{:S(2)}, u32[]{:S(2)}) collective-permute-start(bf16[32,768]{1,0:T(8,128)(2,1)S(1)} %fusion.120), channel_id=1, source_target_pairs={{0,8},{1,9},{2,10},{3,11},{4,12},{5,13},{6,14},{7,15},{8,0},{9,1},... | collective-permute-start | bytes 147464 | tf_op jit(solution)/shard_map/ppermute | solution.py:13
  79.5 4.9 %collective-permute-start.14 = (bf16[32,768]{1,0:T(8,128)(2,1)S(1)}, bf16[32,768]{1,0:T(8,128)(2,1)S(1)}, u32[]{:S(2)}, u32[]{:S(2)}) collective-permute-start(bf16[32,768]{1,0:T(8,128)(2,1)S(1)} %fusion.120), channel_id=1, source_target_pairs={{0,12},{1,13},{2,14},{3,15},{4,0},{5,1},{6,2},{7,3},{8,4},{9,5},{1... | collective-permute-start | bytes 147464 | tf_op jit(solution)/shard_map/ppermute | solution.py:13
  84.5 4.1 %collective-permute-start.20 = (f32[32,768]{1,0:T(8,128)S(1)}, f32[32,768]{1,0:T(8,128)S(1)}, u32[]{:S(2)}, u32[]{:S(2)}) collective-permute-start(f32[32,768]{1,0:T(8,128)S(1)} %convert_add_fusion), channel_id=1, source_target_pairs={{0,2},{1,3},{2,0},{3,1},{4,6},{5,7},{6,4},{7,5},{8,10},{9,11},{10,... | collective-permute-start | bytes 294920 | tf_op jit(solution)/shard_map/ppermute | solution.py:13
  87.2 1.4 %copy-start.2 = (f32[192,3072]{1,0:T(8,128)}, f32[192,3072]{1,0:T(8,128)S(1)}, u32[]{:S(2)}) copy-start(f32[192,3072]{1,0:T(8,128)S(1)} %convolution_add_fusion) | copy-start | bytes 7077892
  88.6 7.5 %collective-permute-start.21 = (f32[32,768]{1,0:T(8,128)S(1)}, f32[32,768]{1,0:T(8,128)S(1)}, u32[]{:S(2)}, u32[]{:S(2)}) collective-permute-start(f32[32,768]{1,0:T(8,128)S(1)} %add.364), channel_id=1, source_target_pairs={{0,1},{1,0},{2,3},{3,2},{4,5},{5,4},{6,7},{7,6},{8,9},{9,8},{10,11... | collective-permute-start | bytes 294920 | tf_op jit(solution)/shard_map/ppermute | solution.py:13
  90.3 9.4 %collective-permute-start.15 = (bf16[48,3072]{1,0:T(8,128)(2,1)S(1)}, bf16[48,3072]{1,0:T(8,128)(2,1)S(1)}, u32[]{:S(2)}, u32[]{:S(2)}) collective-permute-start(bf16[48,3072]{1,0:T(8,128)(2,1)S(1)} %get-tuple-element.38), channel_id=1, source_target_pairs={{0,4},{1,5},{2,6},{3,7},{4,8},{5,9},{6,10},{7,11},{8,12},{9,13},{1... | collective-permute-start | bytes 884744 | tf_op jit(solution)/shard_map/ppermute | solution.py:13
  91.4 25.4 %collective-permute-start.16 = (bf16[48,3072]{1,0:T(8,128)(2,1)S(1)}, bf16[48,3072]{1,0:T(8,128)(2,1)S(1)}, u32[]{:S(2)}, u32[]{:S(2)}) collective-permute-start(bf16[48,3072]{1,0:T(8,128)(2,1)S(1)} %get-tuple-element.40), channel_id=1, source_target_pairs={{0,8},{1,9},{2,10},{3,11},{4,12},{5,13},{6,14},{7,15},{8,0},{9,1},... | collective-permute-start | bytes 884744 | tf_op jit(solution)/shard_map/ppermute | solution.py:13
  94.7 26.4 %collective-permute-start.17 = (bf16[48,3072]{1,0:T(8,128)(2,1)S(1)}, bf16[48,3072]{1,0:T(8,128)(2,1)S(1)}, u32[]{:S(2)}, u32[]{:S(2)}) collective-permute-start(bf16[48,3072]{1,0:T(8,128)(2,1)S(1)} %get-tuple-element.39), channel_id=1, source_target_pairs={{0,12},{1,13},{2,14},{3,15},{4,0},{5,1},{6,2},{7,3},{8,4},{9,5},{1... | collective-permute-start | bytes 884744 | tf_op jit(solution)/shard_map/ppermute | solution.py:13
